TPU v7x, 256 devices: a whole 4x4x8 slice. The times are simulated.
256 devices in a mesh: row: 8 (over y, core), col: 32 (over x, z).
Axes of the slice: x: 4, y: 4, z: 8, core: 2. Of those that a mesh axis runs over, the one named last changes fastest.
Arguments:
- kkt: float32 [8192, 8192], P('row', 'col'), may hold values from -4 to 4, as said below
- swaps: int32 [2, 2, 128], replicated, may hold values from 0 to 8191, as said below
- inverses: float32 [2, 256, 256], replicated
- pivots: float32 [2, 256], replicated, may hold values from -0.12 to 0.12
- couplings: float32 [2, 256], replicated, may hold values from -0.12 to 0.12
- pattern: int32 [2, 256], replicated, may hold values from 0 to 1, as said below
Outputs:
- factored: float32 [8192, 8192], P('row', 'col')
Inputs may be any that keep to these rules, and one draw needn't show every extreme that they name: For panel k, swaps[k, 0, :] holds 128 distinct rows among k * 256 to k * 256 + 255, both ends of that range among them, and swaps[k, 1, :] holds 128 distinct rows among (k + 1) * 256 to 8191, both ends of that range among them. pattern[k, i] = 1 makes rows i and i + 1 one 2 x 2 block of D; no two neighbouring entries are both 1 and the last entry is 0. kkt is the stored order of a symmetric matrix.
All inputs are finite; a program needn't handle non-finite values.
Results may differ from a plain program's by a relative error of at most 0.00014.
Values sent between devices are 32-bit elements; how exact they have to be, the bound alone decides.
A program may use at most 64 MiB of HBM per device.

v0:
```python
import jax
import jax.numpy as jnp
from jax import lax
from jax.sharding import Mesh
from jax.sharding import PartitionSpec as P

COL = ("col_0", "col_1")


highest_prec = lax.Precision.HIGHEST


def from_everyone(shard, axis):
    length = lax.axis_size(axis)
    return lax.all_to_all(
        jnp.broadcast_to(shard[None], (length, *shard.shape)), axis, 0, 0, tiled=True
    )


def over_copies(shard, axis):
    return from_everyone(shard, axis).sum(axis=0)


def from_root(shard, axes, root):
    shard = jnp.where(lax.axis_index(axes) == root, shard, jnp.zeros_like(shard))
    for axis in axes:
        shard = lax.psum(shard, axis)
    return shard


def picked(shard, axis, root):
    return lax.dynamic_index_in_dim(lax.all_gather(shard, axis), root, 0, keepdims=False)


def swap_order(lead_rows, partner_rows, total):
    row_order = jnp.arange(total, dtype=jnp.int32)
    return row_order.at[lead_rows].set(partner_rows).at[partner_rows].set(lead_rows)


def scale_cols(lower_rows, pivot_row, coupling_row, pattern_row):
    links = coupling_row * pattern_row.astype(jnp.float32)
    zero_col = jnp.zeros((lower_rows.shape[0], 1), lower_rows.dtype)
    after = jnp.concatenate([lower_rows[:, 1:], zero_col], axis=1)
    before = jnp.concatenate([zero_col, lower_rows[:, :-1]], axis=1)
    links_before = jnp.concatenate([jnp.zeros((1,), links.dtype), links[:-1]])
    return lower_rows * pivot_row + after * links + before * links_before


def pick_lines(local_block, sources, group_count, my_index, tile_width, along):
    tile_idx = sources // tile_width
    is_owned = tile_idx % group_count == my_index
    local_idx = jnp.where(is_owned, tile_idx // group_count * tile_width + sources % tile_width, 0)
    taken = jnp.take(local_block, local_idx, axis=along)
    if along == 0:
        return jnp.where(is_owned[:, None], taken, 0.0)
    return jnp.where(is_owned[None, :], taken, 0.0)


def place_lines(local_block, targets, arrived, group_count, my_index, tile_width, along):
    tile_idx = targets // tile_width
    is_owned = tile_idx % group_count == my_index
    local_idx = jnp.where(
        is_owned,
        tile_idx // group_count * tile_width + targets % tile_width,
        local_block.shape[along],
    )
    if along == 0:
        return local_block.at[local_idx].set(arrived, mode="drop")
    return local_block.at[:, local_idx].set(arrived, mode="drop")


def shards(kkt, swaps, inverses, pivots, couplings, pattern):
    rows_dev, cols_dev = kkt.shape
    tile_width = inverses.shape[1]
    row_groups = lax.axis_size("row")
    col_groups = lax.axis_size(COL)
    row_index = lax.axis_index("row")
    col_index = lax.axis_index(COL)
    tiles_col = cols_dev // tile_width
    order_len = tiles_col * col_groups * tile_width
    row_positions = jnp.arange(rows_dev, dtype=jnp.int32)
    col_positions = jnp.arange(cols_dev, dtype=jnp.int32)
    row_tiles = row_positions // tile_width * row_groups + row_index
    col_tiles = col_positions // tile_width * col_groups + col_index
    matrix = kkt
    first_order = swap_order(swaps[0, 0], swaps[0, 1], order_len)
    second_order = swap_order(swaps[1, 0], swaps[1, 1], order_len)
    targets = jnp.concatenate([swaps[0, 0], swaps[0, 1], swaps[1, 0], swaps[1, 1]])
    sources = jnp.take(first_order, jnp.take(second_order, targets))
    arrived = over_copies(pick_lines(matrix, sources, row_groups, row_index, tile_width, 0), "row")
    matrix = place_lines(matrix, targets, arrived, row_groups, row_index, tile_width, 0)
    arrived = lax.psum(pick_lines(matrix, sources, col_groups, col_index, tile_width, 1), COL)
    matrix = place_lines(matrix, targets, arrived, col_groups, col_index, tile_width, 1)
    for panel in range(2):
        have_panel = False
        panel_cols = from_root(matrix, COL, panel % col_groups)
        row_tail = row_tiles > panel
        col_tail = col_tiles > panel
        product = jnp.dot(
            panel_cols, inverses[panel], precision=highest_prec, preferred_element_type=jnp.float32
        )
        lower_rows = jnp.where(row_tail[:, None], product, 0.0)
        top_strip = picked(matrix[0:tile_width, :], "row", panel % row_groups)
        strip_product = lax.dot_general(
            top_strip,
            inverses[panel],
            (((0,), (0,)), ((), ())),
            precision=highest_prec,
            preferred_element_type=jnp.float32,
        )
        lower_cols = jnp.where(col_tail[:, None], strip_product, 0.0)
        scaled_cols = scale_cols(lower_cols, pivots[panel], couplings[panel], pattern[panel])
        update = lax.dot_general(
            lower_rows,
            scaled_cols,
            (((1,), (1,)), ((), ())),
            precision=highest_prec,
            preferred_element_type=jnp.float32,
        )
        matrix = matrix - update
        panel_block = jnp.where(
            (col_index == panel % col_groups) & row_tail[:, None], lower_rows, matrix
        )
        matrix = matrix.at[:, 0:tile_width].set(panel_block)
        top_block = jnp.where(
            (row_index == panel % row_groups) & col_tail[None, :],
            scaled_cols.T,
            matrix[0:tile_width, :],
        )
        matrix = matrix.at[0:tile_width, :].set(top_block)
    return matrix


def solution(mesh):
    finer = Mesh(mesh.devices.reshape(mesh.shape["row"], 4, 8), ("row", "col_0", "col_1"))
    in_specs = (P("row", COL), P(), P(), P(), P(), P())
    out_specs = P("row", COL)
    return jax.shard_map(
        shards, mesh=finer, in_specs=in_specs, out_specs=out_specs, check_vma=False
    )
```

profile of v0, /device:TPU:18, one launch (start us, length us, event | category | flops | bytes accessed | tf_op | source)
XLA Modules:
  0.0 580.2 jit_solution(1921041206649546350)
XLA Ops:
  6.5 0.0 copy-start.1
  6.5 1.2 copy.41
  7.8 0.0 copy-done.1
  7.8 1.1 scatter_fusion.2
  8.9 1.1 scatter_fusion.3
  10.0 3.1 gather_fusion.2
  13.2 1.1 scatter_fusion
  14.3 1.1 scatter_fusion.1
  15.3 3.1 gather_fusion.3
  18.6 1.6 gather_fusion
  20.1 0.2 select_select_fusion
  20.4 2.3 broadcast_in_dim.160
  22.7 4.8 all-to-all-start
  27.5 0.0 all-reduce.10.cloned.1.call-start
  27.6 46.5 %all-to-all-done = f32[8,512,256]{2,1,0:T(8,128)} async-done(((f32[8,512,256]{2,1,0:T(8,128)}), f32[8,512,256]{2,1,0:T(8,128)}, u32[]{:S(2)}, u32[]{:S(2)}) %all-to-all-start) | async-done | bytes 4194336 | tf_op jit(solution)/shard_map/all_to_all | solution.py:15
  74.1 2.5 reduce_sum.9
  76.6 2.7 scatter_fusion.4
  79.3 0.3 copy.20
  79.6 2.7 gather_fusion.1
  82.3 3.2 select_bitcast_fusion
  85.5 0.0 all-reduce.10.cloned.1.call-update
  85.5 0.0 all-reduce.12.cloned.1.call-start
  85.6 156.5 %all-reduce.10.cloned.1.call-done = f32[1024,512]{0,1:T(8,128)} async-done(((f32[1024,512]{0,1:T(8,128)}), f32[1024,512]{0,1:T(8,128)}) %all-reduce.10.cloned.1.call-update) | async-done | bytes 2097168 | tf_op jit(solution)/shard_map/psum | solution.py:92
  242.1 4.0 scatter_custom_fusion.5
  246.1 0.3 copy.21
  246.4 0.0 copy-start.2
  246.5 0.0 copy-start.3
  246.5 0.0 copy-start.4
  246.5 1.0 broadcast_select_fusion.1
  247.5 0.0 all-reduce.12.cloned.1.call-update
  247.5 0.0 all-reduce.14.cloned.1.call-start
  247.6 49.5 %all-reduce.12.cloned.1.call-done = f32[1024,256]{1,0:T(8,128)} async-done(((f32[1024,256]{1,0:T(8,128)}), f32[1024,256]{1,0:T(8,128)}) %all-reduce.12.cloned.1.call-update) | async-done | bytes 1048592 | tf_op jit(solution)/shard_map/psum | solution.py:27
  297.1 0.0 all-reduce.14.cloned.1.call-update
  297.1 0.0 all-gather.5.cloned.1.call-start
  297.2 0.7 slice.173
  297.9 0.0 all-gather.5.cloned.1.call-update
  297.9 0.2 all-reduce.16.cloned.1.call-start
  298.2 0.0 copy-done.2
  298.2 0.0 copy-done.3
  298.2 0.1 pad_maximum_fusion.1
  298.3 0.0 copy-done.4
  298.3 78.8 %all-reduce.14.cloned.1.call-done = f32[1024,256]{1,0:T(8,128)} async-done(((f32[1024,256]{1,0:T(8,128)}), f32[1024,256]{1,0:T(8,128)}) %all-reduce.14.cloned.1.call-update) | async-done | bytes 1048592 | tf_op jit(solution)/shard_map/psum | solution.py:27
  377.1 2.2 convolution_select_fusion.1
  379.3 24.8 %all-gather.5.cloned.1.call-done = f32[2048,256]{0,1:T(8,128)} async-done(((f32[256,256]{0,1:T(8,128)}), f32[2048,256]{0,1:T(8,128)}) %all-gather.5.cloned.1.call-update) | async-done | bytes 2097168 | tf_op jit(solution)/shard_map/all_gather | solution.py:32
  404.2 1.6 convolution_select_fusion.3
  405.8 0.2 multiply_add_fusion.1
  406.0 1.0 fusion.3
  407.0 0.8 constant_dynamic-update-slice_fusion
  407.8 1.0 broadcast_select_fusion
  408.8 0.0 all-reduce.16.cloned.1.call-update
  408.8 0.0 all-reduce.18.cloned.1.call-start
  408.9 51.9 %all-reduce.16.cloned.1.call-done = f32[1024,256]{1,0:T(8,128)} async-done(((f32[1024,256]{1,0:T(8,128)}), f32[1024,256]{1,0:T(8,128)}) %all-reduce.16.cloned.1.call-update) | async-done | bytes 1048592 | tf_op jit(solution)/shard_map/psum | solution.py:27
  460.8 0.0 all-reduce.18.cloned.1.call-update
  460.8 0.0 all-gather.7.cloned.1.call-start
  460.8 0.7 all-gather.7.cloned.1.call-update
  461.6 0.1 pad_maximum_fusion
  461.7 78.9 %all-reduce.18.cloned.1.call-done = f32[1024,256]{1,0:T(8,128)} async-done(((f32[1024,256]{1,0:T(8,128)}), f32[1024,256]{1,0:T(8,128)}) %all-reduce.18.cloned.1.call-update) | async-done | bytes 1048592 | tf_op jit(solution)/shard_map/psum | solution.py:27
  540.6 0.0 copy-done
  540.6 2.2 convolution_select_fusion
  542.8 25.1 %all-gather.7.cloned.1.call-done = f32[2048,256]{1,0:T(8,128)} async-done(((f32[256,256]{1,0:T(8,128)}), f32[2048,256]{1,0:T(8,128)}) %all-gather.7.cloned.1.call-update) | async-done | bytes 2097168 | tf_op jit(solution)/shard_map/all_gather | solution.py:32
  567.9 1.5 convolution_select_fusion.2
  569.5 0.2 multiply_add_fusion
  569.7 2.0 fusion.2
  571.6 1.7 fusion.4
  (26 shorter events, 0.3 us)
Async XLA Ops:
  6.5 1.2 copy-start.1
  22.7 51.4 %all-to-all-start = ((f32[8,512,256]{2,1,0:T(8,128)}), f32[8,512,256]{2,1,0:T(8,128)}, u32[]{:S(2)}, u32[]{:S(2)}) async-start(f32[8,512,256]{2,1,0:T(8,128)} %broadcast_in_dim.160), calls=%async_computation | async-start | bytes 8388608 | tf_op jit(solution)/shard_map/all_to_all | solution.py:15
  27.5 214.6 %all-reduce.10.cloned.1.call-start = ((), (), s32[]{:S(2)}) async-start(), calls=%async_computation.1 | async-start | bytes 4194304 | tf_op jit(solution)/shard_map/psum | solution.py:92
  85.5 211.6 %all-reduce.12.cloned.1.call-start = ((), (), s32[]{:S(2)}) async-start(), calls=%async_computation.2 | async-start | bytes 2097152 | tf_op jit(solution)/shard_map/psum | solution.py:27
  246.4 51.7 %copy-start.2 = (s32[2,256]{1,0:T(2,128)S(1)}, s32[2,256]{1,0:T(2,128)}, u32[]{:S(2)}) copy-start(s32[2,256]{1,0:T(2,128)} %param.25) | copy-start | bytes 6148
  246.5 51.7 %copy-start.3 = (f32[2,256]{1,0:T(2,128)S(1)}, f32[2,256]{1,0:T(2,128)}, u32[]{:S(2)}) copy-start(f32[2,256]{1,0:T(2,128)} %param.24) | copy-start | bytes 6148
  246.5 51.8 %copy-start.4 = (f32[2,256]{1,0:T(2,128)S(1)}, f32[2,256]{1,0:T(2,128)}, u32[]{:S(2)}) copy-start(f32[2,256]{1,0:T(2,128)} %param.23) | copy-start | bytes 6148
  247.5 129.5 %all-reduce.14.cloned.1.call-start = ((), (), s32[]{:S(2)}) async-start(), calls=%async_computation.3 | async-start | bytes 2097152 | tf_op jit(solution)/shard_map/psum | solution.py:27
  297.1 107.0 %all-gather.5.cloned.1.call-start = ((), (), s32[]{:S(2)}) async-start(), calls=%async_computation.6 | async-start | bytes 2359296 | tf_op jit(solution)/shard_map/all_gather | solution.py:32
  297.9 162.9 %all-reduce.16.cloned.1.call-start = ((), (), s32[]{:S(2)}) async-start(), calls=%async_computation.4 | async-start | bytes 2097152 | tf_op jit(solution)/shard_map/psum | solution.py:27
  407.8 132.8 %copy-start = (f32[2,256,256]{2,1,0:T(8,128)S(1)}, f32[2,256,256]{2,1,0:T(8,128)}, u32[]{:S(2)}) copy-start(f32[2,256,256]{2,1,0:T(8,128)} %param.22) | copy-start | bytes 1572868
  408.8 131.8 %all-reduce.18.cloned.1.call-start = ((), (), s32[]{:S(2)}) async-start(), calls=%async_computation.5 | async-start | bytes 2097152 | tf_op jit(solution)/shard_map/psum | solution.py:27
  460.8 107.1 %all-gather.7.cloned.1.call-start = ((), (), s32[]{:S(2)}) async-start(), calls=%async_computation.7 | async-start | bytes 2359296 | tf_op jit(solution)/shard_map/all_gather | solution.py:32
Sparse Core Ops, SparseCore 0:
  85.6 156.3 all-reduce.9
  247.7 49.3 all-reduce.11
  299.4 77.5 all-reduce.13
  378.8 25.3 all-gather.4
  409.0 51.7 all-reduce.15
  463.0 77.5 all-reduce.17
  542.5 25.4 all-gather.6
where the time goes:
time: 583 us; the launch traced here: 580 us
  waiting for transfers between devices  513 us (88%)
  local copies, waits for them, and re-layouts  26.5 us (5%)
  between operations  13.9 us (2%)
  other arithmetic  11.2 us (2%)
  matrix products  10.6 us (2%)
    psum x4, waiting for transfers between devices, from_root(): shard = lax.psum(shard, axis)  259 us
    psum x1, waiting for transfers between devices, shards(): lax.psum(pick_lines(matrix, sources, col_groups, col_index, tile_width, 1...  157 us
    all_gather x2, waiting for transfers between devices, picked(): lax.all_gather(shard, axis)  49.9 us
    all_to_all x1, waiting for transfers between devices, from_everyone(): lax.all_to_all(jnp.broadcast_to(shard[None], (length, *shard.shape)), axi...  46.5 us
  transfers between devices with their start and end apart: 8, of which 8 were waited for; matrix products, arithmetic and copies ran while one was open for 1% of the time, Pallas kernels for 0%

commit v1 on v0

v1 whole, which is shorter than its diff:
```python
import jax
import jax.numpy as jnp
from jax import lax
from jax.sharding import Mesh
from jax.sharding import PartitionSpec as P

COL = ("col_0", "col_1")
HI = lax.Precision.HIGHEST


def tdot(a, b):
    return lax.dot_general(
        a, b, (((0,), (0,)), ((), ())), precision=HI, preferred_element_type=jnp.float32
    )


def swapped(rows, lead, partner):
    to_partner = rows[:, None] == lead[None, :]
    to_lead = rows[:, None] == partner[None, :]
    moved = jnp.sum(
        jnp.where(to_partner, partner[None, :], 0) + jnp.where(to_lead, lead[None, :], 0), axis=1
    )
    return jnp.where(jnp.any(to_partner | to_lead, axis=1), moved, rows)


def plan(swaps, tile, row_groups, dtype=jnp.float32):
    width = tile // row_groups
    count = swaps.shape[2]
    partner = swaps[:, 1, :].reshape(-1)
    top = jnp.arange(2 * tile, dtype=jnp.int32)
    rows = jnp.concatenate([top, partner])
    source = swapped(swapped(rows, swaps[1, 0], swaps[1, 1]), swaps[0, 0], swaps[0, 1])
    repeated = jnp.any(swaps[0, 1][:, None] == swaps[1, 1][None, :], axis=1)
    valid = jnp.concatenate([~repeated, jnp.ones((count,), bool)]) & (partner >= 2 * tile)
    sliced = source.reshape(3, row_groups, width).transpose(1, 0, 2)
    return rows, source, sliced, jnp.where(valid, partner, -1)


def hits(rows, first, tile):
    return (rows[:, None] == first + jnp.arange(tile, dtype=jnp.int32)[None, :]).astype(jnp.float32)


def along_d(lower_t, pivot, coupling, pattern):
    links = coupling * pattern.astype(jnp.float32)
    zero = jnp.zeros((1, lower_t.shape[1]), lower_t.dtype)
    after = jnp.concatenate([lower_t[1:], zero], axis=0)
    before = jnp.concatenate([zero, lower_t[:-1]], axis=0)
    links_before = jnp.concatenate([jnp.zeros((1,), links.dtype), links[:-1]])
    return lower_t * pivot[:, None] + after * links[:, None] + before * links_before[:, None]


def exchange(picked, moves, tile, row_groups, x_size):
    width = tile // row_groups
    row_index = lax.axis_index("row")
    z_index = lax.axis_index("col_1")
    piece = lax.psum_scatter(picked, "row", scatter_dimension=0, tiled=False)
    strip = lax.all_gather(piece, "row")
    mine = lax.psum(jnp.where(z_index == row_index, strip, 0.0), "col_1")
    wide = lax.all_gather(mine, "col_0")
    part = jnp.dot(piece, moves, precision=HI, preferred_element_type=jnp.float32)
    t0, t1, tp = part[:width], part[width : 2 * width], part[2 * width :]
    corner = jnp.stack(
        [
            t0[:, 2 * tile :],
            t1[:, 2 * tile :],
            tp[:, 2 * tile :],
            t0[:, tile : 2 * tile],
            t0[:, :tile],
            t1[:, tile : 2 * tile],
        ]
    )
    corner = lax.all_gather(lax.psum(corner, COL), "row")
    return strip, wide, corner


def shards(kkt, swaps, inverses, pivots, couplings, pattern):
    tile = inverses.shape[1]
    row_groups = lax.axis_size("row")
    x_size = lax.axis_size("col_0")
    z_size = lax.axis_size("col_1")
    row_index = lax.axis_index("row")
    col_index = lax.axis_index(COL)
    rows, source, sliced, partner = plan(swaps, tile, row_groups)
    flat = sliced.reshape(-1)
    owned = flat // tile % row_groups == row_index
    taken = jnp.take(kkt, flat // tile // row_groups * tile + flat % tile, axis=0)
    picked = jnp.where(owned[:, None], taken, 0.0).reshape(row_groups, -1, tile)
    moves = hits(source, col_index * tile, tile).T
    strip, wide, corner = exchange(picked, moves, tile, row_groups, x_size)

    def ordered(piece):
        return piece.reshape(row_groups, 3, -1, tile).transpose(1, 0, 2, 3).reshape(-1, tile)

    corner = corner.transpose(1, 0, 2, 3).reshape(6, tile, tile)
    to_partner = corner[0:3].reshape(3 * tile, tile)
    block_01, block_00, block_11 = corner[3], corner[4], corner[5]

    tiles = [row_index + row_groups * slot for slot in range(x_size)] + [col_index]
    strips = [ordered(wide[slot]) for slot in range(x_size)] + [ordered(strip)]
    marks = [hits(partner, index * tile, tile) for index in tiles]
    keep = [1.0 - jnp.sum(mark, axis=0) for mark in marks]
    fixed = [
        strips[n] * keep[n][None, :]
        + jnp.dot(to_partner, marks[n], precision=HI, preferred_element_type=jnp.float32)
        for n in range(x_size + 1)
    ]
    upper = [jnp.where(tiles[n] == 1, block_01, fixed[n][:tile]) for n in range(x_size + 1)]
    low0 = [jnp.where(tiles[n] > 0, tdot(inverses[0], upper[n]), 0.0) for n in range(x_size + 1)]
    low0_1 = tdot(inverses[0], block_01)
    scaled0_1 = along_d(low0_1, pivots[0], couplings[0], pattern[0])
    scaled0 = along_d(low0[-1], pivots[0], couplings[0], pattern[0])
    low1 = [
        jnp.where(
            tiles[n] > 1,
            tdot(inverses[1], fixed[n][tile : 2 * tile] - tdot(scaled0_1, low0[n])),
            0.0,
        )
        for n in range(x_size + 1)
    ]
    scaled1 = along_d(low1[-1], pivots[1], couplings[1], pattern[1])
    outs = []
    for n in range(x_size):
        base = kkt[n * tile : (n + 1) * tile] * keep[n][:, None] * keep[-1][None, :]
        base = base + tdot(marks[n], fixed[-1][2 * tile :])
        base = base + tdot(fixed[n][2 * tile :] * keep[n][None, :], marks[-1])
        value = base - tdot(low0[n], scaled0) - tdot(low1[n], scaled1)
        value = jnp.where(tiles[n] == 0, scaled0, value)
        value = jnp.where(tiles[n] == 1, scaled1, value)
        at_0 = jnp.where(tiles[n] == 0, block_00, low0[n].T)
        at_1 = jnp.where(tiles[n] == 0, scaled0_1, low1[n].T)
        at_1 = jnp.where(tiles[n] == 1, block_11 - tdot(low0_1, scaled0_1), at_1)
        value = jnp.where(col_index == 0, at_0, value)
        value = jnp.where(col_index == 1, at_1, value)
        outs.append(value)
    return jnp.concatenate(outs, axis=0)


def solution(mesh):
    z_size = mesh.shape["row"]
    finer = Mesh(mesh.devices.reshape(mesh.shape["row"], -1, z_size), ("row", "col_0", "col_1"))
    in_specs = (P("row", COL), P(), P(), P(), P(), P())
    return jax.shard_map(
        shards, mesh=finer, in_specs=in_specs, out_specs=P("row", COL), check_vma=False
    )
```

time: 583 us -> 370 us (0.63)
  waiting for transfers between devices: 513 us -> 297 us
  blocking collectives: 0 us -> 17.1 us
  local copies, waits for them, and re-layouts: 26.5 us -> 11.6 us
  matrix products: 10.6 us -> 22.2 us
    psum x5 -> x2, waiting for transfers between devices: 416 us -> 205 us  [the longest x1 130 us: exchange(): corner = lax.all_gather(lax.psum(corner, COL), 'row')]
    all_to_all x1 -> x0, waiting for transfers between devices: 46.5 us -> none  [from_everyone(): lax.all_to_all(jnp.broadcast_to(shard[None], (length, *shard.shape)), axi...]
    reduce_scatter x0 -> x1, waiting for transfers between devices: none -> 32.1 us  [exchange(): piece = lax.psum_scatter(picked, 'row', scatter_dimension=0, tiled=False)]
    all_gather x0 -> x1, blocking collectives: none -> 17.1 us  [exchange(): strip = lax.all_gather(piece, 'row')]
    dot_general x6 -> x39, matrix products: 10.6 us -> 22.2 us  [the longest x33 17.9 us: tdot(): lax.dot_general(a, b, (((0,), (0,)), ((), ())), precision=HI, preferred_e...]
    scatter x8 -> x0, local copies, waits for them, and re-layouts: 11.6 us -> none  [the longest x2 4.34 us: place_lines(): return local_block.at[:, local_idx].set(arrived, mode='drop')]
    all_gather x2, waiting for transfers between devices: 49.9 us -> 60.1 us  [the longest x1 34.5 us: exchange(): wide = lax.all_gather(mine, 'col_0')]
    gather x4 -> x1, local copies, waits for them, and re-layouts: 10.5 us -> 3.33 us  [shards(): jnp.take(kkt, flat // tile // row_groups * tile + flat % tile, axis=0)]
  transfers between devices with their start and end apart: 8 -> 5, of which waited for: 8 -> 5; matrix products, arithmetic and copies ran while one was open for 1% -> 3% of each run, Pallas kernels for 0% -> 0%
where the time goes in v1:
time: 370 us; the launch traced here: 368 us
  waiting for transfers between devices  297 us (80%)
  matrix products  22.2 us (6%)
  blocking collectives  17.1 us (5%)
  between operations  13.9 us (4%)
  local copies, waits for them, and re-layouts  11.6 us (3%)
  other arithmetic  5.64 us (2%)
    psum x1, waiting for transfers between devices, exchange(): corner = lax.all_gather(lax.psum(corner, COL), 'row')  130 us
    psum x1, waiting for transfers between devices, exchange(): mine = lax.psum(jnp.where(z_index == row_index, strip, 0.0), 'col_1')  75 us
    all_gather x1, waiting for transfers between devices, exchange(): wide = lax.all_gather(mine, 'col_0')  34.5 us
    reduce_scatter x1, waiting for transfers between devices, exchange(): piece = lax.psum_scatter(picked, 'row', scatter_dimension=0, tiled=False)  32.1 us
    all_gather x1, waiting for transfers between devices, exchange(): corner = lax.all_gather(lax.psum(corner, COL), 'row')  25.7 us
    dot_general x33, matrix products, tdot(): lax.dot_general(a, b, (((0,), (0,)), ((), ())), precision=HI, preferred_e...  17.9 us
    all_gather x1, blocking collectives, exchange(): strip = lax.all_gather(piece, 'row')  17.1 us
  transfers between devices with their start and end apart: 5, of which 5 were waited for; matrix products, arithmetic and copies ran while one was open for 3% of the time, Pallas kernels for 0%

profile of v1, /device:TPU:18, one launch (start us, length us, event | category | flops | bytes accessed | tf_op | source)
XLA Modules:
  0.0 368.0 jit_solution(7685777161819229525)
XLA Ops:
  6.5 0.8 slice_bitcast_fusion.9
  7.3 0.7 slice.199
  8.0 0.3 fusion.38
  8.3 0.3 fusion.33
  8.6 0.3 fusion.39
  8.9 0.3 fusion.35
  9.6 3.3 gather_fusion
  12.9 1.2 select_select_fusion
  14.2 32.1 %reduce-scatter.2.cloned.1.call-done = f32[1,96,256]{2,1,0:T(8,128)} async-done(((f32[8,96,256]{2,1,0:T(8,128)}), f32[1,96,256]{2,1,0:T(8,128)}) %reduce-scatter.2.cloned.1.call-update) | async-done | bytes 98320 | tf_op jit(solution)/shard_map/reduce_scatter | solution.py:56
  46.3 1.5 fusion.17
  47.9 0.7 copy-done.4
  48.6 17.1 %all_gather.17 = f32[8,96,256]{2,1,0:T(8,128)S(1)} all-gather(f32[1,96,256]{2,1,0:T(8,128)} %reduce-scatter.2.cloned.1.call-done), channel_id=1, replica_groups=mesh['row'=8,'col_0'=4,'col_1'=8] {'row'}, dimensions={0}, use_global_device_ids=true | all-gather | bytes 884736 | tf_op jit(solution)/shard_map/all_gather | solution.py:57
  65.7 1.0 select_bitcast_fusion
  66.7 129.9 %all-reduce.10.cloned.1.call-done = f32[1,6,32,256]{3,2,1,0:T(8,128)} async-done(((f32[1,6,32,256]{3,2,1,0:T(8,128)}), f32[1,6,32,256]{3,2,1,0:T(8,128)}) %all-reduce.10.cloned.1.call-update) | async-done | bytes 196624 | tf_op jit(solution)/shard_map/psum | solution.py:72
  196.7 0.2 all-gather.5.cloned.1.call-start
  197.2 0.2 fusion.40
  197.4 75.0 %all-reduce.12.cloned.1.call-done = f32[1,8,96,256]{3,2,1,0:T(8,128)} async-done(((f32[1,8,96,256]{3,2,1,0:T(8,128)}), f32[1,8,96,256]{3,2,1,0:T(8,128)}) %all-reduce.12.cloned.1.call-update) | async-done | bytes 786448 | tf_op jit(solution)/shard_map/psum | solution.py:58
  272.7 25.7 %all-gather.3.cloned.1.call-done = f32[8,6,32,256]{3,2,1,0:T(8,128)} async-done(((f32[1,6,32,256]{3,2,1,0:T(8,128)}), f32[8,6,32,256]{3,2,1,0:T(8,128)}) %all-gather.3.cloned.1.call-update) | async-done | bytes 1572880 | tf_op jit(solution)/shard_map/all_gather | solution.py:72
  298.3 1.5 copy.51
  299.9 0.8 fusion.125
  300.9 0.6 fusion.55
  301.5 0.6 convolution_add_fusion.3
  302.1 0.6 convolution_select_fusion.7
  302.7 0.2 multiply_add_fusion
  302.9 0.6 convolution_subtract_fusion.11
  303.6 0.6 fusion.8
  304.4 0.4 copy-done
  304.8 1.2 convolution_add_fusion.6
  306.0 0.5 convolution_add_fusion.8
  306.5 0.5 convolution_add_fusion.10
  306.9 0.5 convolution_add_fusion.12
  307.4 0.6 convolution_subtract_fusion.13
  308.0 34.5 %all-gather.5.cloned.1.call-done = f32[4,8,96,256]{3,2,1,0:T(8,128)} async-done(((f32[1,8,96,256]{3,2,1,0:T(8,128)}), f32[4,8,96,256]{3,2,1,0:T(8,128)}) %all-gather.5.cloned.1.call-update) | async-done | bytes 3145744 | tf_op jit(solution)/shard_map/all_gather | solution.py:59
  342.5 2.2 fusion.124
  344.8 0.6 convolution_add_fusion.2
  345.5 0.6 convolution_add_fusion.1
  346.3 0.6 convolution_add_fusion
  347.0 0.6 convolution_add_fusion.4
  347.6 0.4 copy-done.2
  347.9 0.4 convolution_add_fusion.5
  348.4 0.6 convolution_select_fusion.1
  349.0 0.6 convolution_subtract_fusion.2
  349.6 0.4 convolution_add_fusion.7
  350.0 0.6 convolution_select_fusion.3
  350.7 0.8 convolution_subtract_fusion.5
  351.5 0.4 convolution_subtract_fusion.1
  351.9 0.4 convolution_subtract_fusion.4
  352.2 0.4 convolution_add_fusion.9
  352.7 0.6 convolution_select_fusion.5
  353.3 0.6 convolution_subtract_fusion.8
  353.9 0.4 convolution_subtract_fusion.7
  354.3 0.4 convolution_add_fusion.11
  354.8 0.6 bitcast_select_fusion.3
  355.4 0.6 convolution_subtract_fusion.12
  356.0 0.4 convolution_subtract_fusion.10
  356.4 0.6 convolution_select_fusion
  357.0 0.6 convolution_select_fusion.2
  357.6 0.6 convolution_select_fusion.4
  358.2 0.6 convolution_select_fusion.8
  358.8 0.4 fusion.16
  359.2 0.4 fusion.14
  359.6 0.4 fusion.12
  360.0 0.4 fusion.10
  360.4 1.0 pad_maximum_fusion
  (67 shorter events, 2.1 us)
Async XLA Ops:
  6.5 39.8 %reduce-scatter.2.cloned.1.call-start = ((), (), s32[]{:S(2)}) async-start(), calls=%async_computation.1 | async-start | bytes 884736 | tf_op jit(solution)/shard_map/reduce_scatter | solution.py:56
  14.1 182.5 %all-reduce.10.cloned.1.call-start = ((), (), s32[]{:S(2)}) async-start(), calls=%async_computation.2 | async-start | bytes 393216 | tf_op jit(solution)/shard_map/psum | solution.py:72
  47.9 0.7 copy-start.4
  48.6 148.8 %copy-start.5 = (s32[2,256]{1,0:T(2,128)S(1)}, s32[2,256]{1,0:T(2,128)}, u32[]{:S(2)}) copy-start(s32[2,256]{1,0:T(2,128)} %param.11) | copy-start | bytes 6148
  48.6 148.8 %copy-start.6 = (f32[2,256]{1,0:T(2,128)S(1)}, f32[2,256]{1,0:T(2,128)}, u32[]{:S(2)}) copy-start(f32[2,256]{1,0:T(2,128)} %param.10) | copy-start | bytes 6148
  48.6 223.8 %all-reduce.12.cloned.1.call-start = ((), (), s32[]{:S(2)}) async-start(), calls=%async_computation.4 | async-start | bytes 1572864 | tf_op jit(solution)/shard_map/psum | solution.py:58
  65.7 206.8 %copy-start.7 = (f32[2,256]{1,0:T(2,128)S(1)}, f32[2,256]{1,0:T(2,128)}, u32[]{:S(2)}) copy-start(f32[2,256]{1,0:T(2,128)} %param.9) | copy-start | bytes 6148
  66.7 231.6 %all-gather.3.cloned.1.call-start = ((), (), s32[]{:S(2)}) async-start(), calls=%async_computation.3 | async-start | bytes 1769472 | tf_op jit(solution)/shard_map/all_gather | solution.py:72
  196.7 145.9 %all-gather.5.cloned.1.call-start = ((), (), s32[]{:S(2)}) async-start(), calls=%async_computation.5 | async-start | bytes 3932160 | tf_op jit(solution)/shard_map/all_gather | solution.py:59
  299.8 1.0 copy-start.1
  303.5 1.2 copy-start
  347.0 1.0 copy-start.2
  353.3 1.5 copy-start.3
Sparse Core Ops, SparseCore 0:
  14.2 32.0 reduce-scatter.1
  49.7 146.8 all-reduce.9
  199.0 73.3 all-reduce.11
  274.1 24.1 all-gather.2
  300.0 42.5 all-gather.4

commit v2 on v1

--- a/solution.py
+++ b/solution.py
@@ -1,6 +1,10 @@
+import functools
+
 import jax
 import jax.numpy as jnp
 from jax import lax
+from jax.experimental import pallas as pl
+from jax.experimental.pallas import tpu as pltpu
 from jax.sharding import Mesh
 from jax.sharding import PartitionSpec as P
 
@@ -49,28 +53,354 @@
     return lower_t * pivot[:, None] + after * links[:, None] + before * links_before[:, None]
 
 
-def exchange(picked, moves, tile, row_groups, x_size):
-    width = tile // row_groups
-    row_index = lax.axis_index("row")
-    z_index = lax.axis_index("col_1")
-    piece = lax.psum_scatter(picked, "row", scatter_dimension=0, tiled=False)
-    strip = lax.all_gather(piece, "row")
-    mine = lax.psum(jnp.where(z_index == row_index, strip, 0.0), "col_1")
-    wide = lax.all_gather(mine, "col_0")
-    part = jnp.dot(piece, moves, precision=HI, preferred_element_type=jnp.float32)
-    t0, t1, tp = part[:width], part[width : 2 * width], part[2 * width :]
-    corner = jnp.stack(
+MESH = pl.DeviceIdType.MESH
+
+
+def remote(src, dst, send, recv, device):
+    return pltpu.make_async_remote_copy(
+        src_ref=src, dst_ref=dst, send_sem=send, recv_sem=recv, device_id=device, device_id_type=MESH
+    )
+
+
+def exchange_kernel(
+    sizes,
+    picked,
+    moves,
+    strip,
+    wide,
+    corner,
+    special,
+    arrived,
+    shares,
+    share,
+    share_in,
+    cross,
+    summed,
+    rs_send,
+    rs_recv,
+    ag_send,
+    ag_recv,
+    z_send,
+    z_recv,
+    x_send,
+    x_recv,
+    f_send,
+    f_recv,
+    cz_send,
+    cz_recv,
+    cx_send,
+    cx_recv,
+    cg_send,
+    cg_recv,
+    cr_send,
+    cr_recv,
+    sp_send,
+    sp_recv,
+):
+    rows_n, x_n, z_n, width = sizes
+    r = lax.axis_index("row")
+    x = lax.axis_index("col_0")
+    z = lax.axis_index("col_1")
+
+    def row_peer(d):
+        return (lax.rem(r + d, rows_n), x, z)
+
+    def z_peer(d):
+        return (r, x, lax.rem(z + d + z_n, z_n))
+
+    def x_peer(d):
+        return (r, lax.rem(x + d + x_n, x_n), z)
+
+    barrier = pltpu.get_barrier_semaphore()
+    for d in range(1, rows_n):
+        pl.semaphore_signal(barrier, inc=1, device_id=row_peer(d), device_id_type=MESH)
+    for d in range(1, z_n):
+        pl.semaphore_signal(barrier, inc=1, device_id=z_peer(d), device_id_type=MESH)
+    for d in range(1, x_n):
+        pl.semaphore_signal(barrier, inc=1, device_id=x_peer(d), device_id_type=MESH)
+    pl.semaphore_wait(barrier, rows_n + z_n + x_n - 3)
+
+    def reduce_copy(d):
+        return remote(
+            picked.at[lax.rem(r + d, rows_n)],
+            arrived.at[d - 1],
+            rs_send.at[d - 1],
+            rs_recv.at[d - 1],
+            row_peer(d),
+        )
+
+    for d in range(1, rows_n):
+        reduce_copy(d).start()
+    total = picked[r]
+    for d in range(1, rows_n):
+        reduce_copy(d).wait_recv()
+        total = total + arrived[d - 1]
+    strip[r] = total
+
+    def gather_copy(d):
+        return remote(
+            strip.at[r], strip.at[r], ag_send.at[d - 1], ag_recv.at[d - 1], row_peer(d)
+        )
+
+    def gathered(d):
+        q = lax.rem(r - d + rows_n, rows_n)
+        return remote(
+            strip.at[q], strip.at[q], ag_send.at[d - 1], ag_recv.at[d - 1], row_peer(d)
+        )
+
+    for d in range(1, rows_n):
+        gather_copy(d).start()
+
+    offset = lax.rem(z - r + z_n, z_n)
+    half = z_n // 2
+    is_root = offset == 0
+    upward = offset <= half
+    passes = ((offset > 0) & (offset < half)) | (offset > half + 1)
+    ahead = jnp.where(upward, 1, z_n - 1)
+
+    def z_copy(src, q, d, slot, step):
+        return remote(
+            src, wide.at[x, q], z_send.at[slot, d], z_recv.at[d], z_peer(step)
+        )
+
+    def x_copy(src, q, d, side):
+        return remote(
+            src,
+            wide.at[x, q],
+            x_send.at[side, d],
+            x_recv.at[side, d],
+            x_peer(1 if side == 0 else x_n - 1),
+        )
+
+    def f_copy(d, q):
+        if d % 2 == 0:
+            held = wide.at[lax.rem(x + x_n - 1, x_n), q]
+            return remote(held, held, f_send.at[d], f_recv.at[d], x_peer(1))
+        held = wide.at[lax.rem(x + 1, x_n), q]
+        return remote(held, held, f_send.at[d], f_recv.at[d], x_peer(x_n - 1))
+
+    def own_piece(d):
+        q = lax.rem(r - d + rows_n, rows_n)
+
+        @pl.when(is_root)
+        def _():
+            if d > 0:
+                gathered(d).wait_recv()
+            z_copy(strip.at[q], q, d, 0, 1).start()
+            z_copy(strip.at[q], q, d, 1, z_n - 1).start()
+            x_copy(strip.at[q], q, d, 0).start()
+            x_copy(strip.at[q], q, d, 1).start()
+            wide[x, q] = strip[q]
+
+        @pl.when(jnp.logical_not(is_root))
+        def _():
+            z_copy(wide.at[x, q], q, d, 0, ahead).wait_recv()
+
+            @pl.when(passes)
+            def _():
+                z_copy(wide.at[x, q], q, d, 0, ahead).start()
+
+            x_copy(wide.at[x, q], q, d, 0).start()
+            x_copy(wide.at[x, q], q, d, 1).start()
+
+    def side_piece(d):
+        q = lax.rem(r - d + rows_n, rows_n)
+        x_copy(wide.at[x, q], q, d, 0).wait_recv()
+        if d % 2 == 0:
+            f_copy(d, q).start()
+        x_copy(wide.at[x, q], q, d, 1).wait_recv()
+        if d % 2 == 1:
+            f_copy(d, q).start()
+
+    def share_copy(d):
+        return remote(
+            shares.at[lax.rem(z + d, z_n)],
+            share_in.at[d - 1],
+            cz_send.at[d - 1],
+            cz_recv.at[d - 1],
+            z_peer(d),
+        )
+
+    def cross_copy(d):
+        return remote(share, cross.at[d - 1], cx_send.at[d - 1], cx_recv.at[d - 1], x_peer(d))
+
+    def share_back(d):
+        return remote(
+            summed.at[z], summed.at[z], cg_send.at[d - 1], cg_recv.at[d - 1], z_peer(d)
+        )
+
+    def share_taken(d):
+        q = lax.rem(z - d + z_n, z_n)
+        return remote(
+            summed.at[q], summed.at[q], cg_send.at[d - 1], cg_recv.at[d - 1], z_peer(d)
+        )
+
+    own_piece(0)
+
+    part = jnp.dot(
+        strip[r], moves[...], precision=HI, preferred_element_type=jnp.float32
+    )
+    tile = moves.shape[1] // 3
+    blocks = (
+        (0, 2), (1, 2), (2, 2), (0, 1), (0, 0), (1, 1)
+    )
+    stacked = jnp.concatenate(
         [
-            t0[:, 2 * tile :],
-            t1[:, 2 * tile :],
-            tp[:, 2 * tile :],
-            t0[:, tile : 2 * tile],
-            t0[:, :tile],
-            t1[:, tile : 2 * tile],
-        ]
-    )
-    corner = lax.all_gather(lax.psum(corner, COL), "row")
-    return strip, wide, corner
+            part[i * width : (i + 1) * width, j * tile : (j + 1) * tile]
+            for i, j in blocks
+        ],
+        axis=0,
+    )
+    depth = 6 * width // z_n
+    for n in range(z_n):
+        shares[n] = stacked[n * depth : (n + 1) * depth]
+    for d in range(1, z_n):
+        share_copy(d).start()
+
+    own_piece(1)
+    side_piece(0)
+    own_piece(2)
+    side_piece(1)
+
+    value = shares[z]
+    for d in range(1, z_n):
+        share_copy(d).wait_recv()
+        value = value + share_in[d - 1]
+    share[...] = value
+    for d in range(1, x_n):
+        cross_copy(d).start()
+
+    if rows_n > 4:
+        own_piece(3)
+        side_piece(2)
+    for d in range(1, x_n):
+        cross_copy(d).wait_recv()
+        value = value + cross[d - 1]
+    summed[z] = value
+    for d in range(1, z_n):
+        share_back(d).start()
+
+    first = 4 if rows_n > 4 else 3
+    for d in range(first, rows_n):
+        own_piece(d)
+        side_piece(d - 1)
+        if d == rows_n - 2 or rows_n == 4:
+            for e in range(1, z_n):
+                share_taken(e).wait_recv()
+            flat = jnp.concatenate([summed[n] for n in range(z_n)], axis=0)
+            corner[r] = flat[: 4 * width]
+            special[r] = flat[4 * width :]
+            for e in range(1, rows_n):
+                remote(
+                    corner.at[r], corner.at[r], cr_send.at[e - 1], cr_recv.at[e - 1], row_peer(e)
+                ).start()
+            for home in range(2):
+                @pl.when((x == 0) & (z == home) & (r != home))
+                def _():
+                    remote(
+                        special.at[r],
+                        special.at[r],
+                        sp_send,
+                        sp_recv.at[r],
+                        (home, x, z),
+                    ).start()
+    side_piece(rows_n - 1)
+
+    for d in range(1, rows_n):
+        @pl.when(jnp.logical_not(is_root))
+        def _():
+            gathered(d).wait_recv()
+
+        q = lax.rem(r - d + rows_n, rows_n)
+        remote(
+            corner.at[q], corner.at[q], cr_send.at[d - 1], cr_recv.at[d - 1], row_peer(d)
+        ).wait()
+        reduce_copy(d).wait_send()
+        gather_copy(d).wait_send()
+    for d in range(rows_n):
+        q = lax.rem(r - d + rows_n, rows_n)
+        f_copy(d, q).wait()
+        x_copy(wide.at[x, q], q, d, 0).wait_send()
+        x_copy(wide.at[x, q], q, d, 1).wait_send()
+
+        @pl.when(is_root | passes)
+        def _():
+            z_copy(wide.at[x, q], q, d, 0, ahead).wait_send()
+
+        @pl.when(is_root)
+        def _():
+            z_copy(wide.at[x, q], q, d, 1, ahead).wait_send()
+
+    for d in range(1, z_n):
+        share_copy(d).wait_send()
+        share_back(d).wait_send()
+    for d in range(1, x_n):
+        cross_copy(d).wait_send()
+    for home in range(2):
+        for n in range(rows_n):
+            if n != home:
+                here = (x == 0) & (z == home)
+
+                @pl.when(here & (r == n))
+                def _():
+                    remote(
+                        special.at[n], special.at[n], sp_send, sp_recv.at[n], (home, x, z)
+                    ).wait_send()
+
+                @pl.when(here & (r == home))
+                def _():
+                    remote(
+                        special.at[n], special.at[n], sp_send, sp_recv.at[n], (n, x, z)
+                    ).wait_recv()
+
+
+def exchange(picked, moves, tile, rows_n, x_n):
+    z_n = rows_n
+    width = tile // rows_n
+    depth = 6 * width // z_n
+    f32 = jnp.float32
+    dma = pltpu.SemaphoreType.DMA
+    vmem = pl.BlockSpec(memory_space=pltpu.VMEM)
+    return pl.pallas_call(
+        functools.partial(exchange_kernel, (rows_n, x_n, z_n, width)),
+        out_shape=(
+            jax.ShapeDtypeStruct((rows_n, 3 * width, tile), f32),
+            jax.ShapeDtypeStruct((x_n, rows_n, 3 * width, tile), f32),
+            jax.ShapeDtypeStruct((rows_n, 4 * width, tile), f32),
+            jax.ShapeDtypeStruct((rows_n, 2 * width, tile), f32),
+        ),
+        in_specs=[vmem] * 2,
+        out_specs=(vmem,) * 4,
+        scratch_shapes=[
+            pltpu.VMEM((rows_n - 1, 3 * width, tile), f32),
+            pltpu.VMEM((z_n, depth, tile), f32),
+            pltpu.VMEM((depth, tile), f32),
+            pltpu.VMEM((z_n - 1, depth, tile), f32),
+            pltpu.VMEM((x_n - 1, depth, tile), f32),
+            pltpu.VMEM((z_n, depth, tile), f32),
+            dma((rows_n - 1,)),
+            dma((rows_n - 1,)),
+            dma((rows_n - 1,)),
+            dma((rows_n - 1,)),
+            dma((2, rows_n)),
+            dma((rows_n,)),
+            dma((2, rows_n)),
+            dma((2, rows_n)),
+            dma((rows_n,)),
+            dma((rows_n,)),
+            dma((z_n - 1,)),
+            dma((z_n - 1,)),
+            dma((x_n - 1,)),
+            dma((x_n - 1,)),
+            dma((z_n - 1,)),
+            dma((z_n - 1,)),
+            dma((rows_n - 1,)),
+            dma((rows_n - 1,)),
+            dma,
+            dma((rows_n,)),
+        ],
+        compiler_params=pltpu.CompilerParams(collective_id=0, has_side_effects=True),
+    )(picked, moves)
 
 
 def shards(kkt, swaps, inverses, pivots, couplings, pattern):
@@ -86,14 +416,15 @@
     taken = jnp.take(kkt, flat // tile // row_groups * tile + flat % tile, axis=0)
     picked = jnp.where(owned[:, None], taken, 0.0).reshape(row_groups, -1, tile)
     moves = hits(source, col_index * tile, tile).T
-    strip, wide, corner = exchange(picked, moves, tile, row_groups, x_size)
+    strip, wide, corner, special = exchange(picked, moves, tile, row_groups, x_size)
 
     def ordered(piece):
         return piece.reshape(row_groups, 3, -1, tile).transpose(1, 0, 2, 3).reshape(-1, tile)
 
-    corner = corner.transpose(1, 0, 2, 3).reshape(6, tile, tile)
+    corner = corner.reshape(row_groups, 4, -1, tile).transpose(1, 0, 2, 3).reshape(4, tile, tile)
+    special = special.reshape(row_groups, 2, -1, tile).transpose(1, 0, 2, 3).reshape(2, tile, tile)
     to_partner = corner[0:3].reshape(3 * tile, tile)
-    block_01, block_00, block_11 = corner[3], corner[4], corner[5]
+    block_01, block_00, block_11 = corner[3], special[0], special[1]
 
     tiles = [row_index + row_groups * slot for slot in range(x_size)] + [col_index]
     strips = [ordered(wide[slot]) for slot in range(x_size)] + [ordered(strip)]

time: 370 us -> 153 us (0.41)
  waiting for transfers between devices: 297 us -> 0 us
  Pallas kernels: 0 us -> 89 us
  blocking collectives: 17.1 us -> 0 us
  matrix products: 22.2 us -> 39.1 us
  between operations: 13.9 us -> 0.82 us
  local copies, waits for them, and re-layouts: 11.6 us -> 15.3 us
    psum x2 -> x0, waiting for transfers between devices: 205 us -> none  [the longest x1 130 us: exchange(): corner = lax.all_gather(lax.psum(corner, COL), 'row')]
    pallas_call x0 -> x1, Pallas kernels: none -> 89 us  [exchange(): pl.pallas_call(functools.partial(exchange_kernel, (rows_n, x_n, z_n, widt...]
    all_gather x2 -> x0, waiting for transfers between devices: 60.1 us -> none  [the longest x1 34.5 us: exchange(): wide = lax.all_gather(mine, 'col_0')]
    reduce_scatter x1 -> x0, waiting for transfers between devices: 32.1 us -> none  [exchange(): piece = lax.psum_scatter(picked, 'row', scatter_dimension=0, tiled=False)]
    dot_general x33, matrix products: 17.9 us -> 35.3 us  [tdot(): lax.dot_general(a, b, (((0,), (0,)), ((), ())), precision=HI, preferred_e...]
    all_gather x1 -> x0, blocking collectives: 17.1 us -> none  [exchange(): strip = lax.all_gather(piece, 'row')]
  transfers between devices with their start and end apart: 5 -> 0, of which waited for: 5 -> 0; matrix products, arithmetic and copies ran while one was open for 3% -> 0% of each run, Pallas kernels for 0% -> 0%
where the time goes in v2:
time: 153 us; the launch traced here: 151 us
  Pallas kernels  89 us (58%)
  matrix products  39.1 us (26%)
  local copies, waits for them, and re-layouts  15.3 us (10%)
  other arithmetic  6.83 us (4%)
    pallas_call x1, Pallas kernels, exchange(): pl.pallas_call(functools.partial(exchange_kernel, (rows_n, x_n, z_n, widt...  89 us
    dot_general x33, matrix products, tdot(): lax.dot_general(a, b, (((0,), (0,)), ((), ())), precision=HI, preferred_e...  35.3 us
    dot_general x5, matrix products, shards(): jnp.dot(to_partner, marks[n], precision=HI, preferred_element_type=jnp.fl...  3.74 us
    gather x1, local copies, waits for them, and re-layouts, shards(): jnp.take(kkt, flat // tile // row_groups * tile + flat % tile, axis=0)  3.33 us
    slice x1, local copies, waits for them, and re-layouts, shards(): strips = [ordered(wide[slot]) for slot in range(x_size)] + [ordered(strip)]  3.28 us

profile of v2, /device:TPU:18, one launch (start us, length us, event | category | flops | bytes accessed | tf_op | source)
XLA Modules:
  0.0 151.0 jit_solution(17499036642896684795)
XLA Ops:
  0.0 0.8 slice_bitcast_fusion.3
  0.8 0.7 slice.172
  1.5 0.3 fusion.34
  1.8 0.3 fusion.31
  2.1 0.3 fusion.35
  2.4 0.3 fusion.33
  2.8 0.1 reshape.369
  2.9 3.3 %gather_fusion = f32[768,256]{1,0:T(8,128)S(1)} fusion(f32[1024,256]{1,0:T(8,128)} %param.6, s32[1024]{0:T(1024)S(1)} %pad_clamp_fusion), kind=kCustom, calls=%fused_computation | custom fusion | bytes 1575936 | tf_op jit(solution)/shard_map/jit(_take)/gather | solution.py:416
  6.3 0.1 reshape.368
  6.4 1.2 select_select_fusion.picked
  7.6 1.0 compare_convert_fusion.moves
  8.6 89.0 %shard_map.64 = (f32[8,96,256]{2,1,0:T(8,128)}, f32[4,8,96,256]{3,2,1,0:T(8,128)}, f32[8,128,256]{2,1,0:T(8,128)}, f32[8,64,256]{2,1,0:T(8,128)}) custom-call(f32[8,96,256]{2,1,0:T(8,128)} %select_select_fusion.picked, f32[256,768]{1,0:T(8,128)} %compare_convert_fusion.moves), custom_call_target="tpu_custom_call" | custom-call | tf_op jit(solution)/shard_map/pallas_call | solution.py:364
  97.6 1.9 %fusion.114 = (f32[1,8,32,256]{3,2,0,1:T(8,128)}, f32[1,8,32,256]{3,2,0,1:T(8,128)}) fusion(f32[2,8,32,256]{3,2,0,1:T(8,128)} %bitcast.153), kind=kLoop, calls=%fused_computation.234 | loop fusion | bytes 1048576 | tf_op jit(solution)/shard_map/slice | solution.py:427
  99.5 1.3 copy.46
  100.8 3.3 %fusion.113 = (f32[1,8,96,256]{3,2,1,0:T(8,128)}, f32[1,8,96,256]{3,2,1,0:T(8,128)}, f32[1,8,96,256]{3,2,1,0:T(8,128)S(1)}, f32[1,8,96,256]{3,2,1,0:T(8,128)S(1)}) fusion(f32[4,8,96,256]{3,2,1,0:T(8,128)} %get-tuple-element.11), kind=kLoop, calls=%fused_computation.233 | loop fusion | bytes 6291456 | tf_op jit(solution)/shard_map/slice | solution.py:430
  104.1 1.0 copy.31
  105.1 0.2 compare_reduce_fusion
  105.3 0.2 fusion.36
  105.5 1.2 bitcast_multiply_fusion.2
  106.8 0.6 convolution_add_fusion.2
  107.4 0.6 convolution_select_fusion.5
  108.0 0.2 copy-done.8
  108.4 0.6 convolution_add_fusion.1
  109.0 0.6 convolution_select_fusion.3
  109.6 0.3 copy-done.12
  109.9 1.3 copy.33
  111.2 1.5 convolution_add_fusion
  112.7 1.6 %convolution_select_fusion.1 = f32[256,256]{1,0:T(8,128)S(1)} fusion(f32[256,256]{1,0:T(8,128)S(1)} %bitcast.137, f32[768,256]{1,0:T(8,128)} %convolution_add_fusion, f32[2,256,256]{2,1,0:T(8,128)S(1)} %copy-done.1, pred[]{:T(512)S(6)} %gt.39, pred[]{:T(512)S(6)} %eq.245), kind=kOutput, calls=%fused_computation.14 | convolution fusion | flops 201457664 | bytes 1048578 | tf_op jit(solution)/shard_map/dot_general | solution.py:16
  114.5 0.6 convolution_add_fusion.4
  115.1 1.6 %bitcast_select_fusion.3 = (f32[256,256]{1,0:T(8,128)}, f32[256,256]{1,0:T(8,128)}, f32[256,256]{1,0:T(8,128)}, f32[256,256]{1,0:T(8,128)}, f32[256,256]{1,0:T(8,128)}) fusion(f32[1,8,32,256]{3,2,0,1:T(8,128)S(1)} %copy-done.15, pred[]{:T(512)S(6)} %eq.227, f32[256,256]{1,0:T(8,128)S(1)} %convolution_select_fusion.5, pred[]{:T(512)S(6)} %eq.238, ...), kind=kOutput, calls=%fused_computation.111 | convolution fusion | flops 201719808 | bytes 3145734 | tf_op jit(solution)/shard_map/dot_general | solution.py:16
  116.9 0.6 convolution_add_fusion.3
  117.5 0.6 convolution_select_fusion.7
  118.2 0.6 fusion.51
  118.9 0.6 copy-done.2
  119.5 0.2 multiply_add_fusion
  119.7 0.6 convolution_subtract_fusion.11
  120.4 0.6 fusion.8
  121.0 0.2 multiply_add_fusion.1
  121.2 0.5 convolution_add_fusion.6
  121.7 0.4 convolution_add_fusion.5
  122.1 1.1 convolution_subtract_fusion.1
  123.3 1.3 convolution_subtract_fusion.2
  124.6 2.5 %convolution_select_fusion = f32[256,256]{1,0:T(8,128)} fusion(f32[256,256]{1,0:T(8,128)} %convolution_subtract_fusion.2, f32[2,256,256]{2,1,0:T(8,128)S(1)} %copy-done.1, pred[]{:T(512)S(6)} %gt.38), kind=kOutput, calls=%fused_computation.12 | convolution fusion | flops 201392128 | bytes 786433 | tf_op jit(solution)/shard_map/dot_general | solution.py:16
  127.0 1.6 %convolution_subtract_fusion.13 = f32[256,256]{1,0:T(8,128)S(1)} fusion(f32[256,256]{1,0:T(8,128)} %bitcast.151, f32[256,256]{0,1:T(8,128)} %copy-done.2, f32[256,256]{1,0:T(8,128)S(1)} %get-tuple-element.39), kind=kOutput, calls=%fused_computation.46 | convolution fusion | flops 201392128 | bytes 1048576 | tf_op jit(solution)/shard_map/dot_general | solution.py:16
  128.7 2.3 %fusion.16 = f32[256,256]{1,0:T(8,128)} fusion(f32[256,256]{1,0:T(8,128)} %get-tuple-element.27, f32[256,256]{1,0:T(8,128)S(1)} %multiply_add_fusion.1, f32[256,256]{1,0:T(8,128)S(1)} %get-tuple-element.38, f32[256,256]{1,0:T(8,128)} %convolution_subtract_fusion.1, f32[256,256]{1,0:T(8,128)} %convolution_select_fusion, ...), kind=kOutput, calls=%fused_computation.54 | convolution fusion | flops 201785344 | bytes 2097156 | tf_op jit(solution)/shard_map/dot_general | solution.py:16
  131.0 0.5 convolution_add_fusion.8
  131.5 1.4 convolution_add_fusion.7
  132.9 1.1 convolution_subtract_fusion.4
  134.0 2.2 %convolution_subtract_fusion.5 = f32[256,256]{1,0:T(8,128)} fusion(f32[256,256]{1,0:T(8,128)S(1)} %get-tuple-element.39, f32[256,256]{1,0:T(8,128)S(1)} %copy-done.6, f32[768,256]{1,0:T(8,128)} %copy-done.12), kind=kOutput, calls=%fused_computation.22 | convolution fusion | flops 201392128 | bytes 1048576 | tf_op jit(solution)/shard_map/dot_general | solution.py:16
  136.2 1.6 %convolution_select_fusion.2 = f32[256,256]{1,0:T(8,128)S(1)} fusion(f32[256,256]{1,0:T(8,128)} %convolution_subtract_fusion.5, f32[2,256,256]{2,1,0:T(8,128)S(1)} %copy-done.1, pred[]{:T(512)S(6)} %gt.36), kind=kOutput, calls=%fused_computation.21 | convolution fusion | flops 201392128 | bytes 786433 | tf_op jit(solution)/shard_map/dot_general | solution.py:16
  137.8 2.1 %fusion.14 = f32[256,256]{1,0:T(8,128)} fusion(f32[256,256]{1,0:T(8,128)} %get-tuple-element.26, f32[256,256]{1,0:T(8,128)S(1)} %multiply_add_fusion.1, f32[256,256]{1,0:T(8,128)S(1)} %get-tuple-element.38, f32[256,256]{1,0:T(8,128)} %convolution_subtract_fusion.4, f32[256,256]{1,0:T(8,128)S(1)} %convolution_select_fusion.2, ...), kind=kOutput, calls=%fused_computation.52 | convolution fusion | flops 201785344 | bytes 2097156 | tf_op jit(solution)/shard_map/dot_general | solution.py:16
  139.9 0.5 convolution_add_fusion.10
  140.4 0.4 convolution_add_fusion.9
  140.9 1.1 convolution_subtract_fusion.7
  142.0 1.3 convolution_subtract_fusion.8
  143.3 1.6 %convolution_select_fusion.4 = f32[256,256]{1,0:T(8,128)S(1)} fusion(f32[256,256]{1,0:T(8,128)} %convolution_subtract_fusion.8, f32[2,256,256]{2,1,0:T(8,128)S(1)} %copy-done.1, pred[]{:T(512)S(6)} %gt.34), kind=kOutput, calls=%fused_computation.30 | convolution fusion | flops 201392128 | bytes 786433 | tf_op jit(solution)/shard_map/dot_general | solution.py:16
  144.9 2.1 %fusion.12 = f32[256,256]{1,0:T(8,128)} fusion(f32[256,256]{1,0:T(8,128)} %get-tuple-element.25, f32[256,256]{1,0:T(8,128)S(1)} %multiply_add_fusion.1, f32[256,256]{1,0:T(8,128)S(1)} %get-tuple-element.38, f32[256,256]{1,0:T(8,128)} %convolution_subtract_fusion.7, f32[256,256]{1,0:T(8,128)S(1)} %convolution_select_fusion.4, ...), kind=kOutput, calls=%fused_computation.50 | convolution fusion | flops 201785344 | bytes 2097156 | tf_op jit(solution)/shard_map/dot_general | solution.py:16
  147.0 0.5 convolution_add_fusion.12
  147.5 0.4 convolution_add_fusion.11
  148.0 0.4 convolution_subtract_fusion.10
  148.3 0.6 convolution_subtract_fusion.12
  149.0 0.6 convolution_select_fusion.8
  149.6 0.4 fusion.10
  150.0 1.0 pad_maximum_fusion
  (77 shorter events, 1.0 us)
Async XLA Ops:
  105.1 2.3 %copy-start.1 = (f32[2,256,256]{2,1,0:T(8,128)S(1)}, f32[2,256,256]{2,1,0:T(8,128)}, u32[]{:S(2)}) copy-start(f32[2,256,256]{2,1,0:T(8,128)} %param.8) | copy-start | bytes 1572868
  107.4 0.9 copy-start.8
  108.0 7.0 %copy-start.3 = (f32[256,256]{1,0:T(8,128)}, f32[256,256]{1,0:T(8,128)S(1)}, u32[]{:S(2)}) copy-start(f32[256,256]{1,0:T(8,128)S(1)} %convolution_select_fusion.5) | copy-start | bytes 786436
  109.0 0.9 copy-start.12
  109.6 5.4 %copy-start.5 = (f32[256,256]{1,0:T(8,128)}, f32[256,256]{1,0:T(8,128)S(1)}, u32[]{:S(2)}) copy-start(f32[256,256]{1,0:T(8,128)S(1)} %convolution_select_fusion.3) | copy-start | bytes 786436
  109.9 4.4 %copy-start.7 = (f32[1,8,96,256]{3,2,1,0:T(8,128)S(1)}, f32[1,8,96,256]{3,2,1,0:T(8,128)}, u32[]{:S(2)}) copy-start(f32[1,8,96,256]{3,2,1,0:T(8,128)} %get-tuple-element.18) | copy-start | bytes 2359300
  112.7 2.4 %copy-start.15 = (f32[1,8,32,256]{3,2,0,1:T(8,128)S(1)}, f32[1,8,32,256]{3,2,0,1:T(8,128)}, u32[]{:S(2)}) copy-start(f32[1,8,32,256]{3,2,0,1:T(8,128)} %get-tuple-element.23) | copy-start | bytes 786436
  115.0 1.8 %copy-start.10 = (f32[768,256]{1,0:T(8,128)}, f32[768,256]{1,0:T(8,128)S(1)}, u32[]{:S(2)}) copy-start(f32[768,256]{1,0:T(8,128)S(1)} %convolution_add_fusion.4) | copy-start | bytes 2359300
  115.1 1.6 %copy-start.19 = (f32[8,96,256]{2,1,0:T(8,128)S(1)}, f32[8,96,256]{2,1,0:T(8,128)}, u32[]{:S(2)}) copy-start(f32[8,96,256]{2,1,0:T(8,128)} %get-tuple-element.12) | copy-start | bytes 2359300
  116.8 1.3 copy-start.20
  116.8 1.3 copy-start.21
  116.8 1.4 copy-start.22
  118.8 0.7 copy-start.2
  118.9 2.3 %copy-start = (f32[1024,256]{1,0:T(8,128)S(1)}, f32[1024,256]{1,0:T(8,128)}, u32[]{:S(2)}) copy-start(f32[1024,256]{1,0:T(8,128)} %param.6) | copy-start | bytes 3145732
  120.4 1.3 copy-start.13
  128.7 4.2 %copy-start.6 = (f32[256,256]{1,0:T(8,128)S(1)}, f32[256,256]{1,0:T(8,128)}, u32[]{:S(2)}) copy-start(f32[256,256]{1,0:T(8,128)} %copy-done.5) | copy-start | bytes 786436
  136.2 4.2 %copy-start.9 = (f32[768,256]{1,0:T(8,128)S(1)}, f32[768,256]{1,0:T(8,128)}, u32[]{:S(2)}) copy-start(f32[768,256]{1,0:T(8,128)} %copy-done.8) | copy-start | bytes 2359300
  136.2 4.7 %copy-start.4 = (f32[256,256]{1,0:T(8,128)S(1)}, f32[256,256]{1,0:T(8,128)}, u32[]{:S(2)}) copy-start(f32[256,256]{1,0:T(8,128)} %copy-done.3) | copy-start | bytes 786436
  143.2 4.2 %copy-start.11 = (f32[768,256]{1,0:T(8,128)S(1)}, f32[768,256]{1,0:T(8,128)}, u32[]{:S(2)}) copy-start(f32[768,256]{1,0:T(8,128)} %copy-done.10) | copy-start | bytes 2359300
  143.3 4.7 %copy-start.14 = (f32[256,256]{1,0:T(8,128)S(1)}, f32[256,256]{1,0:T(8,128)}, u32[]{:S(2)}) copy-start(f32[256,256]{1,0:T(8,128)} %get-tuple-element.46) | copy-start | bytes 786436
  147.5 2.5 %copy-start.16 = (f32[256,256]{1,0:T(8,128)S(1)}, f32[256,256]{1,0:T(8,128)}, u32[]{:S(2)}) copy-start(f32[256,256]{1,0:T(8,128)} %fusion.16) | copy-start | bytes 786436
  147.5 2.5 %copy-start.17 = (f32[256,256]{1,0:T(8,128)S(1)}, f32[256,256]{1,0:T(8,128)}, u32[]{:S(2)}) copy-start(f32[256,256]{1,0:T(8,128)} %fusion.14) | copy-start | bytes 786436
  147.5 2.5 %copy-start.18 = (f32[256,256]{1,0:T(8,128)S(1)}, f32[256,256]{1,0:T(8,128)}, u32[]{:S(2)}) copy-start(f32[256,256]{1,0:T(8,128)} %fusion.12) | copy-start | bytes 786436

commit v3 on v2

--- a/solution.py
+++ b/solution.py
@@ -10,12 +10,6 @@
 
 COL = ("col_0", "col_1")
 HI = lax.Precision.HIGHEST
-
-
-def tdot(a, b):
-    return lax.dot_general(
-        a, b, (((0,), (0,)), ((), ())), precision=HI, preferred_element_type=jnp.float32
-    )
 
 
 def swapped(rows, lead, partner):
@@ -42,15 +36,6 @@
 
 def hits(rows, first, tile):
     return (rows[:, None] == first + jnp.arange(tile, dtype=jnp.int32)[None, :]).astype(jnp.float32)
-
-
-def along_d(lower_t, pivot, coupling, pattern):
-    links = coupling * pattern.astype(jnp.float32)
-    zero = jnp.zeros((1, lower_t.shape[1]), lower_t.dtype)
-    after = jnp.concatenate([lower_t[1:], zero], axis=0)
-    before = jnp.concatenate([zero, lower_t[:-1]], axis=0)
-    links_before = jnp.concatenate([jnp.zeros((1,), links.dtype), links[:-1]])
-    return lower_t * pivot[:, None] + after * links[:, None] + before * links_before[:, None]
 
 
 MESH = pl.DeviceIdType.MESH
@@ -403,6 +388,163 @@
     )(picked, moves)
 
 
+BF = jnp.bfloat16
+
+
+def halves(a):
+    high = a.astype(BF)
+    return high, (a - high.astype(jnp.float32)).astype(BF)
+
+
+def dot_n(a, b, dims):
+    return lax.dot_general(a, b, (dims, ((), ())), preferred_element_type=jnp.float32)
+
+
+def dot3(a, b, dims):
+    return dot_n(a[0], b[0], dims) + (dot_n(a[0], b[1], dims) + dot_n(a[1], b[0], dims))
+
+
+NN = ((1,), (0,))
+TN = ((0,), (0,))
+
+
+def update_kernel(
+    kkt,
+    wide,
+    strip,
+    corner,
+    special,
+    inverses,
+    pivots,
+    couplings,
+    pattern,
+    partner_col,
+    partner_row,
+    out,
+    coef,
+):
+    x_n, rows_n, deep, tile = wide.shape
+    width = deep // 3
+    r = lax.axis_index("row")
+    c = lax.axis_index("col_0") * lax.axis_size("col_1") + lax.axis_index("col_1")
+    lanes = lax.broadcasted_iota(jnp.int32, (2, tile), 1)
+    links = couplings[...] * pattern[...].astype(jnp.float32)
+    links = jnp.where(lanes == tile - 1, 0.0, links)
+    coef[...] = jnp.zeros_like(coef)
+    coef[0:2, :] = pivots[...]
+    coef[2:4, :] = links
+    coef[4:6, :] = jnp.where(lanes == 0, 0.0, pltpu.roll(links, 1, 1))
+    table = coef[...].T
+
+    def along_d(lower_t, panel):
+        pivot = table[:, panel : panel + 1]
+        after = table[:, 2 + panel : 3 + panel]
+        before = table[:, 4 + panel : 5 + panel]
+        return (
+            lower_t * pivot
+            + pltpu.roll(lower_t, tile - 1, 0) * after
+            + pltpu.roll(lower_t, 1, 0) * before
+        )
+
+    def rows_of(ref, part):
+        return jnp.concatenate(
+            [ref[q, part * width : (part + 1) * width, :] for q in range(rows_n)], axis=0
+        )
+
+    tiles = [r + rows_n * slot for slot in range(x_n)] + [c]
+    inv0 = halves(inverses[0].T)
+    inv1 = halves(inverses[1].T)
+    block_01 = rows_of(corner, 3)
+    low0_1 = dot3(inv0, halves(block_01), NN)
+    scaled0_1 = along_d(low0_1, 0)
+    scaled0_1_rows = halves(scaled0_1.T)
+    to_partner = [halves(rows_of(corner, part)) for part in range(3)]
+    columns = lax.broadcasted_iota(jnp.int32, (tile, tile), 1)
+    depths = lax.broadcasted_iota(jnp.int32, (tile, tile), 0)
+
+    def panels(n):
+        ref = strip if n == x_n else wide.at[n]
+        index = tiles[n]
+        hit = (partner_col[...] - index * tile) == columns
+        mark = jnp.where(hit, 1.0, 0.0).astype(BF)
+        keep = 1.0 - jnp.sum(jnp.where(hit, 1.0, 0.0), axis=0, keepdims=True)
+        fixed = [
+            rows_of(ref, part) * keep
+            + dot_n(to_partner[part][0], mark, NN)
+            + dot_n(to_partner[part][1], mark, NN)
+            for part in range(3)
+        ]
+        upper = jnp.where(index == 1, block_01, fixed[0])
+        low0 = dot3(inv0, halves(upper), NN) * jnp.where(index > 0, 1.0, 0.0)
+        below = fixed[1] - dot3(scaled0_1_rows, halves(low0), NN)
+        low1 = dot3(inv1, halves(below), NN) * jnp.where(index > 1, 1.0, 0.0)
+        return low0, low1, fixed[2], mark, keep
+
+    low0_c, low1_c, moved_c, mark_c, keep_c = panels(x_n)
+    scaled0 = along_d(low0_c, 0)
+    scaled1 = along_d(low1_c, 1)
+    scaled0_h = halves(scaled0)
+    scaled1_h = halves(scaled1)
+    moved_h = halves(moved_c)
+
+    for n in range(x_n):
+        low0, low1, moved, mark, keep = panels(n)
+        place = slice(n * tile, (n + 1) * tile)
+
+        @pl.when(c > 1)
+        def _():
+            hit = (partner_row[...] - tiles[n] * tile) == depths
+            keep_rows = 1.0 - jnp.sum(jnp.where(hit, 1.0, 0.0), axis=1, keepdims=True)
+            value = kkt[place, :] * keep_rows * keep_c
+            value = value + dot_n(mark, moved_h[0], TN) + dot_n(mark, moved_h[1], TN)
+            across = halves(moved * keep)
+            value = value + dot_n(across[0], mark_c, TN) + dot_n(across[1], mark_c, TN)
+            value = value - dot3(halves(low0), scaled0_h, TN)
+            value = value - dot3(halves(low1), scaled1_h, TN)
+            if n == 0:
+                value = jnp.where(r == 0, scaled0, jnp.where(r == 1, scaled1, value))
+            out[place, :] = value
+
+        @pl.when(c == 0)
+        def _():
+            value = low0.T
+            if n == 0:
+                value = jnp.where(r == 0, rows_of(special, 0), value)
+            out[place, :] = value
+
+        @pl.when(c == 1)
+        def _():
+            value = low1.T
+            if n == 0:
+                first = rows_of(special, 1) - dot3(halves(low0_1), halves(scaled0_1), TN)
+                value = jnp.where(r == 0, scaled0_1, jnp.where(r == 1, first, value))
+            out[place, :] = value
+
+
+def update(kkt, wide, strip, corner, special, inverses, pivots, couplings, pattern, partner):
+    tile = kkt.shape[1]
+    vmem = pl.BlockSpec(memory_space=pltpu.VMEM)
+    return pl.pallas_call(
+        update_kernel,
+        out_shape=jax.ShapeDtypeStruct(kkt.shape, jnp.float32),
+        in_specs=[vmem] * 11,
+        out_specs=vmem,
+        scratch_shapes=[pltpu.VMEM((128, tile), jnp.float32)],
+    )(
+        kkt,
+        wide,
+        strip,
+        corner,
+        special,
+        inverses,
+        pivots,
+        couplings,
+        pattern,
+        partner[:, None],
+        partner[None, :],
+    )
+
+
 def shards(kkt, swaps, inverses, pivots, couplings, pattern):
     tile = inverses.shape[1]
     row_groups = lax.axis_size("row")
@@ -418,52 +560,9 @@
     moves = hits(source, col_index * tile, tile).T
     strip, wide, corner, special = exchange(picked, moves, tile, row_groups, x_size)
 
-    def ordered(piece):
-        return piece.reshape(row_groups, 3, -1, tile).transpose(1, 0, 2, 3).reshape(-1, tile)
-
-    corner = corner.reshape(row_groups, 4, -1, tile).transpose(1, 0, 2, 3).reshape(4, tile, tile)
-    special = special.reshape(row_groups, 2, -1, tile).transpose(1, 0, 2, 3).reshape(2, tile, tile)
-    to_partner = corner[0:3].reshape(3 * tile, tile)
-    block_01, block_00, block_11 = corner[3], special[0], special[1]
-
-    tiles = [row_index + row_groups * slot for slot in range(x_size)] + [col_index]
-    strips = [ordered(wide[slot]) for slot in range(x_size)] + [ordered(strip)]
-    marks = [hits(partner, index * tile, tile) for index in tiles]
-    keep = [1.0 - jnp.sum(mark, axis=0) for mark in marks]
-    fixed = [
-        strips[n] * keep[n][None, :]
-        + jnp.dot(to_partner, marks[n], precision=HI, preferred_element_type=jnp.float32)
-        for n in range(x_size + 1)
-    ]
-    upper = [jnp.where(tiles[n] == 1, block_01, fixed[n][:tile]) for n in range(x_size + 1)]
-    low0 = [jnp.where(tiles[n] > 0, tdot(inverses[0], upper[n]), 0.0) for n in range(x_size + 1)]
-    low0_1 = tdot(inverses[0], block_01)
-    scaled0_1 = along_d(low0_1, pivots[0], couplings[0], pattern[0])
-    scaled0 = along_d(low0[-1], pivots[0], couplings[0], pattern[0])
-    low1 = [
-        jnp.where(
-            tiles[n] > 1,
-            tdot(inverses[1], fixed[n][tile : 2 * tile] - tdot(scaled0_1, low0[n])),
-            0.0,
-        )
-        for n in range(x_size + 1)
-    ]
-    scaled1 = along_d(low1[-1], pivots[1], couplings[1], pattern[1])
-    outs = []
-    for n in range(x_size):
-        base = kkt[n * tile : (n + 1) * tile] * keep[n][:, None] * keep[-1][None, :]
-        base = base + tdot(marks[n], fixed[-1][2 * tile :])
-        base = base + tdot(fixed[n][2 * tile :] * keep[n][None, :], marks[-1])
-        value = base - tdot(low0[n], scaled0) - tdot(low1[n], scaled1)
-        value = jnp.where(tiles[n] == 0, scaled0, value)
-        value = jnp.where(tiles[n] == 1, scaled1, value)
-        at_0 = jnp.where(tiles[n] == 0, block_00, low0[n].T)
-        at_1 = jnp.where(tiles[n] == 0, scaled0_1, low1[n].T)
-        at_1 = jnp.where(tiles[n] == 1, block_11 - tdot(low0_1, scaled0_1), at_1)
-        value = jnp.where(col_index == 0, at_0, value)
-        value = jnp.where(col_index == 1, at_1, value)
-        outs.append(value)
-    return jnp.concatenate(outs, axis=0)
+    return update(
+        kkt, wide, strip, corner, special, inverses, pivots, couplings, pattern, partner
+    )
 
 
 def solution(mesh):

time: 153 us -> 112 us (0.73)
  matrix products: 39.1 us -> 0 us
  Pallas kernels: 89 us -> 102 us
  local copies, waits for them, and re-layouts: 15.3 us -> 5.83 us
  other arithmetic: 6.83 us -> 3.69 us
    dot_general x38 -> x0, matrix products: 39.1 us -> none  [the longest x33 35.3 us: tdot(): lax.dot_general(a, b, (((0,), (0,)), ((), ())), precision=HI, preferred_e...]
    pallas_call x0 -> x1, Pallas kernels: none -> 12.7 us  [update(): pl.pallas_call(update_kernel, out_shape=jax.ShapeDtypeStruct(kkt.shape, j...]
    slice x8 -> x0, local copies, waits for them, and re-layouts: 5.37 us -> none  [the longest x1 3.28 us: shards(): strips = [ordered(wide[slot]) for slot in range(x_size)] + [ordered(strip)]]
    transpose x5 -> x0, local copies, waits for them, and re-layouts: 2.38 us -> none  [ordered(): piece.reshape(row_groups, 3, -1, tile).transpose(1, 0, 2, 3)]
where the time goes in v3:
time: 112 us; the launch traced here: 111 us
  Pallas kernels  102 us (91%)
  local copies, waits for them, and re-layouts  5.83 us (5%)
  other arithmetic  3.69 us (3%)
    pallas_call x1, Pallas kernels, exchange(): pl.pallas_call(functools.partial(exchange_kernel, (rows_n, x_n, z_n, widt...  89 us
    pallas_call x1, Pallas kernels, update(): pl.pallas_call(update_kernel, out_shape=jax.ShapeDtypeStruct(kkt.shape, j...  12.7 us
    gather x1, local copies, waits for them, and re-layouts, shards(): jnp.take(kkt, flat // tile // row_groups * tile + flat % tile, axis=0)  3.33 us

profile of v3, /device:TPU:18, one launch (start us, length us, event | category | flops | bytes accessed | tf_op | source)
XLA Modules:
  0.0 111.3 jit_solution(3211632975370654998)
XLA Ops:
  0.0 0.8 slice_bitcast_fusion.3
  0.8 0.7 slice.17
  1.5 0.3 fusion.1
  1.8 0.3 fusion.4
  2.1 0.3 fusion.3
  2.4 0.3 fusion.5
  2.7 0.1 select_n.135
  2.8 0.1 reshape.254
  2.9 0.1 fusion.12
  2.9 3.3 %gather_fusion = f32[768,256]{1,0:T(8,128)S(1)} fusion(f32[1024,256]{1,0:T(8,128)} %kkt.1, s32[1024]{0:T(1024)S(1)} %pad_clamp_fusion), kind=kCustom, calls=%fused_computation | custom fusion | bytes 1575936 | tf_op jit(solution)/shard_map/jit(_take)/gather | solution.py:558
  6.3 0.1 reshape.253
  6.4 1.2 %select_select_fusion.picked = f32[8,96,256]{2,1,0:T(8,128)} fusion(f32[8,96,256]{2,1,0:T(8,128)S(1)} %bitcast.13, pred[8,96]{1,0:T(8,128)(4,1)S(1)} %get-tuple-element.14, pred[8,96]{1,0:T(8,128)(4,1)S(1)} %get-tuple-element.13), kind=kLoop, calls=%fused_computation.1 | loop fusion | flops 393216 | bytes 1574400 | tf_op jit(solution)/shard_map/jit(_where)/select_n | solution.py:559
  7.5 1.0 compare_convert_fusion.moves
  8.6 89.0 %shard_map.64 = (f32[8,96,256]{2,1,0:T(8,128)}, f32[4,8,96,256]{3,2,1,0:T(8,128)}, f32[8,128,256]{2,1,0:T(8,128)}, f32[8,64,256]{2,1,0:T(8,128)}) custom-call(f32[8,96,256]{2,1,0:T(8,128)} %select_select_fusion.picked, f32[256,768]{1,0:T(8,128)} %compare_convert_fusion.moves), custom_call_target="tpu_custom_call" | custom-call | tf_op jit(solution)/shard_map/pallas_call | solution.py:349
  97.6 0.2 compare_reduce_fusion
  97.8 0.0 copy-start
  97.8 0.8 copy.12.partner_col
  98.6 0.0 copy-done
  98.6 12.7 %shard_map.65 = f32[1024,256]{1,0:T(8,128)} custom-call(f32[1024,256]{1,0:T(8,128)} %kkt.1, f32[4,8,96,256]{3,2,1,0:T(8,128)} %get-tuple-element.9.wide, f32[8,96,256]{2,1,0:T(8,128)} %get-tuple-element.10.strip, f32[8,128,256]{2,1,0:T(8,128)} %get-tuple-element.11.corner, f32[8,64,256]{2,1,0:T(8,128)} %get-tuple-element.12.special, ...), custom_call_target="tpu_custom_call" | custom-call | tf_op jit(solution)/shard_map/pallas_call | solution.py:527
  (10 shorter events, 0.1 us)
Async XLA Ops:
  97.8 0.8 copy-start

commit v4 on v3

--- a/solution.py
+++ b/solution.py
@@ -30,7 +30,7 @@
     source = swapped(swapped(rows, swaps[1, 0], swaps[1, 1]), swaps[0, 0], swaps[0, 1])
     repeated = jnp.any(swaps[0, 1][:, None] == swaps[1, 1][None, :], axis=1)
     valid = jnp.concatenate([~repeated, jnp.ones((count,), bool)]) & (partner >= 2 * tile)
-    sliced = source.reshape(3, row_groups, width).transpose(1, 0, 2)
+    sliced = source.reshape(3, row_groups // 2, 2, width).transpose(2, 1, 0, 3)
     return rows, source, sliced, jnp.where(valid, partner, -1)
 
 
@@ -55,16 +55,22 @@
     wide,
     corner,
     special,
-    arrived,
+    near_in,
+    chip_sum,
+    far_in,
     shares,
     share,
     share_in,
     cross,
     summed,
-    rs_send,
-    rs_recv,
-    ag_send,
-    ag_recv,
+    p_send,
+    p_recv,
+    r_send,
+    r_recv,
+    g_send,
+    g_recv,
+    h_send,
+    h_recv,
     z_send,
     z_recv,
     x_send,
@@ -79,16 +85,22 @@
     cg_recv,
     cr_send,
     cr_recv,
+    ch_send,
+    ch_recv,
     sp_send,
     sp_recv,
 ):
-    rows_n, x_n, z_n, width = sizes
+    y_n, x_n, z_n, width = sizes
+    rows_n = 2 * y_n
     r = lax.axis_index("row")
     x = lax.axis_index("col_0")
     z = lax.axis_index("col_1")
-
-    def row_peer(d):
-        return (lax.rem(r + d, rows_n), x, z)
+    y = r // 2
+    k = lax.rem(r, 2)
+    twin = (r + 1 - 2 * k, x, z)
+
+    def y_peer(d):
+        return (lax.rem(r + 2 * d, rows_n), x, z)
 
     def z_peer(d):
         return (r, x, lax.rem(z + d + z_n, z_n))
@@ -96,106 +108,135 @@
     def x_peer(d):
         return (r, lax.rem(x + d + x_n, x_n), z)
 
+    def owner(d, flip):
+        core = k if flip == 0 else 1 - k
+        return 2 * lax.rem(y - d + y_n, y_n) + core
+
     barrier = pltpu.get_barrier_semaphore()
-    for d in range(1, rows_n):
-        pl.semaphore_signal(barrier, inc=1, device_id=row_peer(d), device_id_type=MESH)
+    pl.semaphore_signal(barrier, inc=1, device_id=twin, device_id_type=MESH)
+    for d in range(1, y_n):
+        pl.semaphore_signal(barrier, inc=1, device_id=y_peer(d), device_id_type=MESH)
     for d in range(1, z_n):
         pl.semaphore_signal(barrier, inc=1, device_id=z_peer(d), device_id_type=MESH)
     for d in range(1, x_n):
         pl.semaphore_signal(barrier, inc=1, device_id=x_peer(d), device_id_type=MESH)
-    pl.semaphore_wait(barrier, rows_n + z_n + x_n - 3)
-
-    def reduce_copy(d):
+    for d in range(1, y_n):
+        there = (2 * lax.rem(y + d, y_n) + 1 - k, x, z)
+        pl.semaphore_signal(barrier, inc=1, device_id=there, device_id_type=MESH)
+    pl.semaphore_wait(barrier, 2 * y_n + z_n + x_n - 3)
+
+    def chip_copy(d):
+        n = lax.rem(y + d, y_n)
+        return remote(picked.at[1 - k, n], near_in.at[d], p_send.at[d], p_recv.at[d], twin)
+
+    def y_copy(d):
         return remote(
-            picked.at[lax.rem(r + d, rows_n)],
-            arrived.at[d - 1],
-            rs_send.at[d - 1],
-            rs_recv.at[d - 1],
-            row_peer(d),
-        )
-
-    for d in range(1, rows_n):
-        reduce_copy(d).start()
-    total = picked[r]
-    for d in range(1, rows_n):
-        reduce_copy(d).wait_recv()
-        total = total + arrived[d - 1]
+            chip_sum.at[d - 1], far_in.at[d - 1], r_send.at[d - 1], r_recv.at[d - 1], y_peer(d)
+        )
+
+    order = [2, 1, 3, 0] if y_n == 4 else list(range(1, y_n)) + [0]
+    for d in order:
+        chip_copy(d).start()
+    for d in order[:-1]:
+        chip_copy(d).wait_recv()
+        chip_sum[d - 1] = picked[k, lax.rem(y + d, y_n)] + near_in[d]
+        y_copy(d).start()
+    chip_copy(0).wait_recv()
+    total = picked[k, y] + near_in[0]
+    for d in range(1, y_n):
+        y_copy(d).wait_recv()
+        total = total + far_in[d - 1]
     strip[r] = total
 
-    def gather_copy(d):
-        return remote(
-            strip.at[r], strip.at[r], ag_send.at[d - 1], ag_recv.at[d - 1], row_peer(d)
-        )
-
-    def gathered(d):
-        q = lax.rem(r - d + rows_n, rows_n)
-        return remote(
-            strip.at[q], strip.at[q], ag_send.at[d - 1], ag_recv.at[d - 1], row_peer(d)
-        )
-
-    for d in range(1, rows_n):
-        gather_copy(d).start()
+    def gather_copy(ref, d, send, recv):
+        return remote(ref.at[r], ref.at[r], send.at[d - 1], recv.at[d - 1], y_peer(d))
+
+    def gathered(ref, d, send, recv):
+        q = owner(d, 0)
+        return remote(ref.at[q], ref.at[q], send.at[d - 1], recv.at[d - 1], y_peer(d))
+
+    def twin_copy(ref, d, flip, send, recv):
+        q = owner(d, flip)
+        return remote(ref.at[q], ref.at[q], send.at[d], recv.at[d], twin)
+
+    for d in range(1, y_n):
+        gather_copy(strip, d, g_send, g_recv).start()
+    twin_copy(strip, 0, 0, h_send, h_recv).start()
 
     offset = lax.rem(z - r + z_n, z_n)
     half = z_n // 2
     is_root = offset == 0
+    not_root = jnp.logical_not(is_root)
     upward = offset <= half
     passes = ((offset > 0) & (offset < half)) | (offset > half + 1)
     ahead = jnp.where(upward, 1, z_n - 1)
-
-    def z_copy(src, q, d, slot, step):
+    reach = jnp.minimum(offset, z_n - offset)
+    is_near = reach <= 1
+    is_mid = reach == 2
+    is_far = reach > 2
+    cut = 3 * width // 2
+    if y_n == 4:
+        turn = [(0, 0), (0, 1), (1, 0), (3, 0), (1, 1), (3, 1), (2, 0), (2, 1)]
+    else:
+        turn = [(d, flip) for d in range(y_n) for flip in range(2)]
+    pieces = 2 * rows_n
+
+    def spot(i):
+        q = owner(*turn[i // 2])
+        return q, pl.ds((i % 2) * cut, cut)
+
+    def z_copy(src, i, slot, step):
+        q, part = spot(i)
         return remote(
-            src, wide.at[x, q], z_send.at[slot, d], z_recv.at[d], z_peer(step)
-        )
-
-    def x_copy(src, q, d, side):
+            src.at[q, part], wide.at[x, q, part], z_send.at[slot, i], z_recv.at[i], z_peer(step)
+        )
+
+    def x_copy(src, i, side):
+        q, part = spot(i)
         return remote(
-            src,
-            wide.at[x, q],
-            x_send.at[side, d],
-            x_recv.at[side, d],
+            src.at[q, part],
+            wide.at[x, q, part],
+            x_send.at[side, i],
+            x_recv.at[side, i],
             x_peer(1 if side == 0 else x_n - 1),
         )
 
-    def f_copy(d, q):
-        if d % 2 == 0:
-            held = wide.at[lax.rem(x + x_n - 1, x_n), q]
-            return remote(held, held, f_send.at[d], f_recv.at[d], x_peer(1))
-        held = wide.at[lax.rem(x + 1, x_n), q]
-        return remote(held, held, f_send.at[d], f_recv.at[d], x_peer(x_n - 1))
-
-    def own_piece(d):
-        q = lax.rem(r - d + rows_n, rows_n)
+    def f_copy(i):
+        q, part = spot(i)
+        step = 1 if i % 2 == 0 else x_n - 1
+        held = wide.at[lax.rem(x + x_n - step, x_n), q, part]
+        return remote(held, held, f_send.at[i], f_recv.at[i], x_peer(step))
+
+    def own_piece(i):
+        q, part = spot(i)
+        d, flip = turn[i // 2]
 
         @pl.when(is_root)
         def _():
-            if d > 0:
-                gathered(d).wait_recv()
-            z_copy(strip.at[q], q, d, 0, 1).start()
-            z_copy(strip.at[q], q, d, 1, z_n - 1).start()
-            x_copy(strip.at[q], q, d, 0).start()
-            x_copy(strip.at[q], q, d, 1).start()
-            wide[x, q] = strip[q]
-
-        @pl.when(jnp.logical_not(is_root))
-        def _():
-            z_copy(wide.at[x, q], q, d, 0, ahead).wait_recv()
+            if i % 2 == 0 and flip == 1:
+                twin_copy(strip, d, 1, h_send, h_recv).wait_recv()
+            z_copy(strip, i, 0, 1).start()
+            z_copy(strip, i, 1, z_n - 1).start()
+            x_copy(strip, i, 0).start()
+            x_copy(strip, i, 1).start()
+            wide[x, q, part] = strip[q, part]
+
+        @pl.when(not_root)
+        def _():
+            z_copy(wide.at[x], i, 0, ahead).wait_recv()
 
             @pl.when(passes)
             def _():
-                z_copy(wide.at[x, q], q, d, 0, ahead).start()
-
-            x_copy(wide.at[x, q], q, d, 0).start()
-            x_copy(wide.at[x, q], q, d, 1).start()
-
-    def side_piece(d):
-        q = lax.rem(r - d + rows_n, rows_n)
-        x_copy(wide.at[x, q], q, d, 0).wait_recv()
-        if d % 2 == 0:
-            f_copy(d, q).start()
-        x_copy(wide.at[x, q], q, d, 1).wait_recv()
-        if d % 2 == 1:
-            f_copy(d, q).start()
+                z_copy(wide.at[x], i, 0, ahead).start()
+
+            x_copy(wide.at[x], i, 0).start()
+            x_copy(wide.at[x], i, 1).start()
+
+    def side_piece(i):
+        for side in (i % 2, 1 - i % 2):
+            x_copy(wide.at[x], i, side).wait_recv()
+            if side == i % 2:
+                f_copy(i).start()
 
     def share_copy(d):
         return remote(
@@ -220,15 +261,72 @@
             summed.at[q], summed.at[q], cg_send.at[d - 1], cg_recv.at[d - 1], z_peer(d)
         )
 
-    own_piece(0)
-
-    part = jnp.dot(
-        strip[r], moves[...], precision=HI, preferred_element_type=jnp.float32
-    )
+    def corner_z():
+        value = shares[z]
+        for d in range(1, z_n):
+            share_copy(d).wait_recv()
+            value = value + share_in[d - 1]
+        share[...] = value
+        for d in range(1, x_n):
+            cross_copy(d).start()
+
+    def corner_x():
+        value = share[...]
+        for d in range(1, x_n):
+            cross_copy(d).wait_recv()
+            value = value + cross[d - 1]
+        summed[z] = value
+        for d in range(1, z_n):
+            share_back(d).start()
+
+    def corner_back():
+        for d in range(1, z_n):
+            share_taken(d).wait_recv()
+        flat = jnp.concatenate([summed[n] for n in range(z_n)], axis=0)
+        corner[r] = flat[: 4 * width]
+        special[r] = flat[4 * width :]
+        for d in range(1, y_n):
+            gather_copy(corner, d, cr_send, cr_recv).start()
+        twin_copy(corner, 0, 0, ch_send, ch_recv).start()
+        for home in range(2):
+            @pl.when((x == 0) & (z == home) & (r != home))
+            def _():
+                remote(
+                    special.at[r], special.at[r], sp_send, sp_recv.at[r], (home, x, z)
+                ).start()
+
+    def corner_twin():
+        for d in range(1, y_n):
+            gathered(corner, d, cr_send, cr_recv).wait_recv()
+            twin_copy(corner, d, 0, ch_send, ch_recv).start()
+
+    steps = [corner_z, corner_x, corner_back, corner_twin]
+    spots = {True: [[3, 5, 11, 14], [1, 3, 9, 13], [-1, -1, 6, 11]], False: [[2, 3, 5, 6]] * 3}
+    spots = spots[pieces == 16]
+
+    def corner_steps(i):
+        for kind, at in zip((is_near, is_mid, is_far), spots):
+            if i in at:
+
+                @pl.when(kind)
+                def _():
+                    for step, place in zip(steps, at):
+                        if place == i:
+                            step()
+
+    @pl.when(is_root)
+    def _():
+        for i in range(2):
+            q, part = spot(i)
+            z_copy(strip, i, 0, 1).start()
+            z_copy(strip, i, 1, z_n - 1).start()
+            x_copy(strip, i, 0).start()
+            x_copy(strip, i, 1).start()
+            wide[x, q, part] = strip[q, part]
+
+    part = jnp.dot(strip[r], moves[...], precision=HI, preferred_element_type=jnp.float32)
     tile = moves.shape[1] // 3
-    blocks = (
-        (0, 2), (1, 2), (2, 2), (0, 1), (0, 0), (1, 1)
-    )
+    blocks = ((0, 2), (1, 2), (2, 2), (0, 1), (0, 0), (1, 1))
     stacked = jnp.concatenate(
         [
             part[i * width : (i + 1) * width, j * tile : (j + 1) * tile]
@@ -242,79 +340,59 @@
     for d in range(1, z_n):
         share_copy(d).start()
 
-    own_piece(1)
-    side_piece(0)
-    own_piece(2)
-    side_piece(1)
-
-    value = shares[z]
-    for d in range(1, z_n):
-        share_copy(d).wait_recv()
-        value = value + share_in[d - 1]
-    share[...] = value
-    for d in range(1, x_n):
-        cross_copy(d).start()
-
-    if rows_n > 4:
-        own_piece(3)
-        side_piece(2)
-    for d in range(1, x_n):
-        cross_copy(d).wait_recv()
-        value = value + cross[d - 1]
-    summed[z] = value
-    for d in range(1, z_n):
-        share_back(d).start()
-
-    first = 4 if rows_n > 4 else 3
-    for d in range(first, rows_n):
-        own_piece(d)
-        side_piece(d - 1)
-        if d == rows_n - 2 or rows_n == 4:
-            for e in range(1, z_n):
-                share_taken(e).wait_recv()
-            flat = jnp.concatenate([summed[n] for n in range(z_n)], axis=0)
-            corner[r] = flat[: 4 * width]
-            special[r] = flat[4 * width :]
-            for e in range(1, rows_n):
-                remote(
-                    corner.at[r], corner.at[r], cr_send.at[e - 1], cr_recv.at[e - 1], row_peer(e)
-                ).start()
-            for home in range(2):
-                @pl.when((x == 0) & (z == home) & (r != home))
+    for d in (1, 3, 2) if y_n == 4 else range(1, y_n):
+        gathered(strip, d, g_send, g_recv).wait_recv()
+        twin_copy(strip, d, 0, h_send, h_recv).start()
+
+    corner_steps(-1)
+    lag = 2
+    for i in range(pieces):
+        if i > 1:
+            own_piece(i)
+        else:
+
+            @pl.when(not_root)
+            def _():
+                z_copy(wide.at[x], i, 0, ahead).wait_recv()
+
+                @pl.when(passes)
                 def _():
-                    remote(
-                        special.at[r],
-                        special.at[r],
-                        sp_send,
-                        sp_recv.at[r],
-                        (home, x, z),
-                    ).start()
-    side_piece(rows_n - 1)
-
-    for d in range(1, rows_n):
-        @pl.when(jnp.logical_not(is_root))
-        def _():
-            gathered(d).wait_recv()
-
-        q = lax.rem(r - d + rows_n, rows_n)
-        remote(
-            corner.at[q], corner.at[q], cr_send.at[d - 1], cr_recv.at[d - 1], row_peer(d)
-        ).wait()
-        reduce_copy(d).wait_send()
-        gather_copy(d).wait_send()
-    for d in range(rows_n):
-        q = lax.rem(r - d + rows_n, rows_n)
-        f_copy(d, q).wait()
-        x_copy(wide.at[x, q], q, d, 0).wait_send()
-        x_copy(wide.at[x, q], q, d, 1).wait_send()
+                    z_copy(wide.at[x], i, 0, ahead).start()
+
+                x_copy(wide.at[x], i, 0).start()
+                x_copy(wide.at[x], i, 1).start()
+
+        corner_steps(i)
+        if i >= lag:
+            side_piece(i - lag)
+    for i in range(pieces - lag, pieces):
+        side_piece(i)
+
+    for d in range(y_n):
+        @pl.when(not_root)
+        def _():
+            twin_copy(strip, d, 1, h_send, h_recv).wait_recv()
+
+        twin_copy(strip, d, 0, h_send, h_recv).wait_send()
+        twin_copy(corner, d, 1, ch_send, ch_recv).wait_recv()
+        twin_copy(corner, d, 0, ch_send, ch_recv).wait_send()
+        chip_copy(d).wait_send()
+    for d in range(1, y_n):
+        y_copy(d).wait_send()
+        gather_copy(strip, d, g_send, g_recv).wait_send()
+        gather_copy(corner, d, cr_send, cr_recv).wait_send()
+    for i in range(pieces):
+        f_copy(i).wait()
+        x_copy(wide.at[x], i, 0).wait_send()
+        x_copy(wide.at[x], i, 1).wait_send()
 
         @pl.when(is_root | passes)
         def _():
-            z_copy(wide.at[x, q], q, d, 0, ahead).wait_send()
+            z_copy(wide.at[x], i, 0, ahead).wait_send()
 
         @pl.when(is_root)
         def _():
-            z_copy(wide.at[x, q], q, d, 1, ahead).wait_send()
+            z_copy(wide.at[x], i, 1, ahead).wait_send()
 
     for d in range(1, z_n):
         share_copy(d).wait_send()
@@ -341,13 +419,14 @@
 
 def exchange(picked, moves, tile, rows_n, x_n):
     z_n = rows_n
+    y_n = rows_n // 2
     width = tile // rows_n
     depth = 6 * width // z_n
     f32 = jnp.float32
     dma = pltpu.SemaphoreType.DMA
     vmem = pl.BlockSpec(memory_space=pltpu.VMEM)
     return pl.pallas_call(
-        functools.partial(exchange_kernel, (rows_n, x_n, z_n, width)),
+        functools.partial(exchange_kernel, (y_n, x_n, z_n, width)),
         out_shape=(
             jax.ShapeDtypeStruct((rows_n, 3 * width, tile), f32),
             jax.ShapeDtypeStruct((x_n, rows_n, 3 * width, tile), f32),
@@ -357,30 +436,38 @@
         in_specs=[vmem] * 2,
         out_specs=(vmem,) * 4,
         scratch_shapes=[
-            pltpu.VMEM((rows_n - 1, 3 * width, tile), f32),
+            pltpu.VMEM((y_n, 3 * width, tile), f32),
+            pltpu.VMEM((y_n - 1, 3 * width, tile), f32),
+            pltpu.VMEM((y_n - 1, 3 * width, tile), f32),
             pltpu.VMEM((z_n, depth, tile), f32),
             pltpu.VMEM((depth, tile), f32),
             pltpu.VMEM((z_n - 1, depth, tile), f32),
             pltpu.VMEM((x_n - 1, depth, tile), f32),
             pltpu.VMEM((z_n, depth, tile), f32),
-            dma((rows_n - 1,)),
-            dma((rows_n - 1,)),
-            dma((rows_n - 1,)),
-            dma((rows_n - 1,)),
-            dma((2, rows_n)),
-            dma((rows_n,)),
-            dma((2, rows_n)),
-            dma((2, rows_n)),
-            dma((rows_n,)),
-            dma((rows_n,)),
+            dma((y_n,)),
+            dma((y_n,)),
+            dma((y_n - 1,)),
+            dma((y_n - 1,)),
+            dma((y_n - 1,)),
+            dma((y_n - 1,)),
+            dma((y_n,)),
+            dma((y_n,)),
+            dma((2, 2 * rows_n)),
+            dma((2 * rows_n,)),
+            dma((2, 2 * rows_n)),
+            dma((2, 2 * rows_n)),
+            dma((2 * rows_n,)),
+            dma((2 * rows_n,)),
             dma((z_n - 1,)),
             dma((z_n - 1,)),
             dma((x_n - 1,)),
             dma((x_n - 1,)),
             dma((z_n - 1,)),
             dma((z_n - 1,)),
-            dma((rows_n - 1,)),
-            dma((rows_n - 1,)),
+            dma((y_n - 1,)),
+            dma((y_n - 1,)),
+            dma((y_n,)),
+            dma((y_n,)),
             dma,
             dma((rows_n,)),
         ],
@@ -405,7 +492,6 @@
 
 
 NN = ((1,), (0,))
-TN = ((0,), (0,))
 
 
 def update_kernel(
@@ -483,9 +569,11 @@
     low0_c, low1_c, moved_c, mark_c, keep_c = panels(x_n)
     scaled0 = along_d(low0_c, 0)
     scaled1 = along_d(low1_c, 1)
-    scaled0_h = halves(scaled0)
-    scaled1_h = halves(scaled1)
-    moved_h = halves(moved_c)
+    scaled0_rows = halves(scaled0.T)
+    scaled1_rows = halves(scaled1.T)
+    moved_rows = halves(moved_c.T)
+    hit_c = (partner_row[...] - c * tile) == depths
+    mark_rows = jnp.where(hit_c, 1.0, 0.0).astype(BF)
 
     for n in range(x_n):
         low0, low1, moved, mark, keep = panels(n)
@@ -495,12 +583,12 @@
         def _():
             hit = (partner_row[...] - tiles[n] * tile) == depths
             keep_rows = 1.0 - jnp.sum(jnp.where(hit, 1.0, 0.0), axis=1, keepdims=True)
-            value = kkt[place, :] * keep_rows * keep_c
-            value = value + dot_n(mark, moved_h[0], TN) + dot_n(mark, moved_h[1], TN)
             across = halves(moved * keep)
-            value = value + dot_n(across[0], mark_c, TN) + dot_n(across[1], mark_c, TN)
-            value = value - dot3(halves(low0), scaled0_h, TN)
-            value = value - dot3(halves(low1), scaled1_h, TN)
+            change = dot_n(moved_rows[0], mark, NN) + dot_n(moved_rows[1], mark, NN)
+            change = change + dot_n(mark_rows, across[0], NN) + dot_n(mark_rows, across[1], NN)
+            change = change - dot3(scaled0_rows, halves(low0), NN)
+            change = change - dot3(scaled1_rows, halves(low1), NN)
+            value = kkt[place, :] * keep_rows * keep_c + change.T
             if n == 0:
                 value = jnp.where(r == 0, scaled0, jnp.where(r == 1, scaled1, value))
             out[place, :] = value
@@ -516,7 +604,7 @@
         def _():
             value = low1.T
             if n == 0:
-                first = rows_of(special, 1) - dot3(halves(low0_1), halves(scaled0_1), TN)
+                first = rows_of(special, 1) - dot3(scaled0_1_rows, halves(low0_1), NN).T
                 value = jnp.where(r == 0, scaled0_1, jnp.where(r == 1, first, value))
             out[place, :] = value
 
@@ -556,7 +644,7 @@
     flat = sliced.reshape(-1)
     owned = flat // tile % row_groups == row_index
     taken = jnp.take(kkt, flat // tile // row_groups * tile + flat % tile, axis=0)
-    picked = jnp.where(owned[:, None], taken, 0.0).reshape(row_groups, -1, tile)
+    picked = jnp.where(owned[:, None], taken, 0.0).reshape(2, row_groups // 2, -1, tile)
     moves = hits(source, col_index * tile, tile).T
     strip, wide, corner, special = exchange(picked, moves, tile, row_groups, x_size)
 

time: 112 us -> 99.9 us (0.89); the launches traced: 111 us -> 97.9 us
  Pallas kernels: 102 us -> 88.3 us
    pallas_call x1, Pallas kernels: 89 us -> 75.5 us  [exchange(): pl.pallas_call(functools.partial(exchange_kernel, (y_n, x_n, z_n, width))...]
where the time goes in v4:
time: 99.9 us; the launch traced here: 97.9 us
  Pallas kernels  88.3 us (88%)
  local copies, waits for them, and re-layouts  5.84 us (6%)
  other arithmetic  3.69 us (4%)
    pallas_call x1, Pallas kernels, exchange(): pl.pallas_call(functools.partial(exchange_kernel, (y_n, x_n, z_n, width))...  75.5 us
    pallas_call x1, Pallas kernels, update(): pl.pallas_call(update_kernel, out_shape=jax.ShapeDtypeStruct(kkt.shape, j...  12.8 us
    gather x1, local copies, waits for them, and re-layouts, shards(): jnp.take(kkt, flat // tile // row_groups * tile + flat % tile, axis=0)  3.33 us

profile of v4, /device:TPU:18, one launch (start us, length us, event | category | flops | bytes accessed | tf_op | source)
XLA Modules:
  0.0 97.9 jit_solution(17055474801228971520)
XLA Ops:
  0.0 0.8 slice_bitcast_fusion.3
  0.8 0.7 slice.17
  1.5 0.3 fusion.1
  1.8 0.3 fusion.4
  2.1 0.3 fusion.3
  2.4 0.3 fusion.5
  2.7 0.1 select_n.135
  2.8 0.1 reshape.254
  2.9 0.1 fusion.12
  2.9 3.3 %gather_fusion = f32[768,256]{1,0:T(8,128)S(1)} fusion(f32[1024,256]{1,0:T(8,128)} %kkt.1, s32[1024]{0:T(1024)S(1)} %pad_clamp_fusion), kind=kCustom, calls=%fused_computation | custom fusion | bytes 1575936 | tf_op jit(solution)/shard_map/jit(_take)/gather | solution.py:646
  6.3 0.1 reshape.253
  6.4 1.2 %select_select_fusion.picked = f32[2,4,96,256]{3,2,1,0:T(8,128)} fusion(f32[2,4,96,256]{3,2,1,0:T(8,128)S(1)} %bitcast.13, pred[2,4,96]{2,1,0:T(4,128)(4,1)S(1)} %get-tuple-element.14, pred[2,4,96]{2,1,0:T(4,128)(4,1)S(1)} %get-tuple-element.13), kind=kLoop, calls=%fused_computation.1 | loop fusion | flops 393216 | bytes 1574400 | tf_op jit(solution)/shard_map/jit(_where)/select_n | solution.py:647
  7.6 1.0 %compare_convert_fusion.moves = f32[256,768]{1,0:T(8,128)} fusion(s32[768]{0:T(1024)S(1)} %select_n.134, s32[256]{0:T(256)S(1)} %iota_add_fusion), kind=kLoop, calls=%fused_computation.2 | loop fusion | flops 393216 | bytes 790528 | tf_op jit(solution)/shard_map/convert_element_type | solution.py:38
  8.6 75.5 %shard_map.64 = (f32[8,96,256]{2,1,0:T(8,128)}, f32[4,8,96,256]{3,2,1,0:T(8,128)}, f32[8,128,256]{2,1,0:T(8,128)}, f32[8,64,256]{2,1,0:T(8,128)}) custom-call(f32[2,4,96,256]{3,2,1,0:T(8,128)} %select_select_fusion.picked, f32[256,768]{1,0:T(8,128)} %compare_convert_fusion.moves), custom_call_target="tpu_custom_call" | custom-call | tf_op jit(solution)/shard_map/pallas_call | solution.py:428
  84.1 0.2 compare_reduce_fusion
  84.3 0.0 copy-start
  84.3 0.8 copy.12.partner_col
  85.1 0.0 copy-done
  85.1 12.8 %shard_map.65 = f32[1024,256]{1,0:T(8,128)} custom-call(f32[1024,256]{1,0:T(8,128)} %kkt.1, f32[4,8,96,256]{3,2,1,0:T(8,128)} %get-tuple-element.9.wide, f32[8,96,256]{2,1,0:T(8,128)} %get-tuple-element.10.strip, f32[8,128,256]{2,1,0:T(8,128)} %get-tuple-element.11.corner, f32[8,64,256]{2,1,0:T(8,128)} %get-tuple-element.12.special, ...), custom_call_target="tpu_custom_call" | custom-call | tf_op jit(solution)/shard_map/pallas_call | solution.py:615
  (10 shorter events, 0.1 us)
Async XLA Ops:
  84.3 0.8 copy-start

commit v5 on v4

--- a/solution.py
+++ b/solution.py
@@ -9,33 +9,32 @@
 from jax.sharding import PartitionSpec as P
 
 COL = ("col_0", "col_1")
-HI = lax.Precision.HIGHEST
+BF = jnp.bfloat16
+F32 = jnp.float32
+NN = ((1,), (0,))
+NT = ((1,), (1,))
+
+
+def halves(a):
+    high = a.astype(BF)
+    return high, (a - high.astype(F32)).astype(BF)
+
+
+def dot_n(a, b, dims):
+    return lax.dot_general(a, b, (dims, ((), ())), preferred_element_type=F32)
+
+
+def dot3(a, b):
+    return dot_n(a[0], b[0], NN) + (dot_n(a[0], b[1], NN) + dot_n(a[1], b[0], NN))
 
 
 def swapped(rows, lead, partner):
-    to_partner = rows[:, None] == lead[None, :]
-    to_lead = rows[:, None] == partner[None, :]
-    moved = jnp.sum(
-        jnp.where(to_partner, partner[None, :], 0) + jnp.where(to_lead, lead[None, :], 0), axis=1
-    )
-    return jnp.where(jnp.any(to_partner | to_lead, axis=1), moved, rows)
-
-
-def plan(swaps, tile, row_groups, dtype=jnp.float32):
-    width = tile // row_groups
-    count = swaps.shape[2]
-    partner = swaps[:, 1, :].reshape(-1)
-    top = jnp.arange(2 * tile, dtype=jnp.int32)
-    rows = jnp.concatenate([top, partner])
-    source = swapped(swapped(rows, swaps[1, 0], swaps[1, 1]), swaps[0, 0], swaps[0, 1])
-    repeated = jnp.any(swaps[0, 1][:, None] == swaps[1, 1][None, :], axis=1)
-    valid = jnp.concatenate([~repeated, jnp.ones((count,), bool)]) & (partner >= 2 * tile)
-    sliced = source.reshape(3, row_groups // 2, 2, width).transpose(2, 1, 0, 3)
-    return rows, source, sliced, jnp.where(valid, partner, -1)
-
-
-def hits(rows, first, tile):
-    return (rows[:, None] == first + jnp.arange(tile, dtype=jnp.int32)[None, :]).astype(jnp.float32)
+    to_partner = rows == lead
+    to_lead = rows == partner
+    moved = jnp.where(to_partner, partner, 0.0) + jnp.where(to_lead, lead, 0.0)
+    touched = jnp.where(to_partner | to_lead, 1.0, 0.0)
+    moved = jnp.sum(moved, axis=1, keepdims=True)
+    return jnp.where(jnp.sum(touched, axis=1, keepdims=True) > 0.0, moved, rows)
 
 
 MESH = pl.DeviceIdType.MESH
@@ -47,10 +46,17 @@
     )
 
 
-def exchange_kernel(
+def step_kernel(
     sizes,
+    kkt,
+    swaps,
+    inverses,
+    pivots,
+    couplings,
+    pattern,
+    out,
+    coef,
     picked,
-    moves,
     strip,
     wide,
     corner,
@@ -123,6 +129,53 @@
     for d in range(1, y_n):
         there = (2 * lax.rem(y + d, y_n) + 1 - k, x, z)
         pl.semaphore_signal(barrier, inc=1, device_id=there, device_id_type=MESH)
+
+    c = x * z_n + z
+    tile = inverses.shape[1]
+    count = tile // 2
+    lanes = lax.broadcasted_iota(jnp.int32, (2, tile), 1)
+    links = couplings[...] * pattern[...].astype(F32)
+    links = jnp.where(lanes == tile - 1, 0.0, links)
+    swap_rows = swaps[...].astype(F32)
+    coef[...] = jnp.zeros_like(coef)
+    coef[0:2, :] = pivots[...]
+    coef[2:4, :] = links
+    coef[4:6, :] = jnp.where(lanes == 0, 0.0, pltpu.roll(links, 1, 1))
+    coef[8:12, 0:count] = swap_rows
+    table = coef[...].T
+    lead_0, partner_0 = swap_rows[0:1], swap_rows[1:2]
+    lead_1, partner_1 = swap_rows[2:3], swap_rows[3:4]
+    partner_0c, partner_1c = table[:count, 9:10], table[:count, 11:12]
+    top = lax.broadcasted_iota(jnp.int32, (2 * tile, 1), 0).astype(F32)
+    rows = jnp.concatenate([top, partner_0c, partner_1c], axis=0)
+    source = swapped(swapped(rows, lead_1, partner_1), lead_0, partner_0)
+    again_c = jnp.sum(jnp.where(partner_0c == partner_1, 1.0, 0.0), axis=1, keepdims=True)
+    again_r = jnp.sum(jnp.where(partner_1c == partner_0, 1.0, 0.0), axis=0, keepdims=True)
+    partner_col = jnp.concatenate([jnp.where(again_c > 0.0, -1.0, partner_0c), partner_1c], axis=0)
+    partner_row = jnp.concatenate([jnp.where(again_r > 0.0, -1.0, partner_0), partner_1], axis=1)
+    partner_col = jnp.where(partner_col < 2 * tile, -1.0, partner_col)
+    partner_row = jnp.where(partner_row < 2 * tile, -1.0, partner_row)
+    columns = lax.broadcasted_iota(jnp.int32, (tile, tile), 1).astype(F32)
+    depths = lax.broadcasted_iota(jnp.int32, (tile, tile), 0).astype(F32)
+    across = lax.broadcasted_iota(jnp.int32, (3 * tile, tile), 1).astype(F32)
+
+    def first_of(index):
+        return (index * tile).astype(F32)
+
+    taken = jnp.zeros((3 * tile, tile), F32)
+    for n in range(x_n):
+        hit = (source - first_of(r + rows_n * n)) == across
+        mark = jnp.where(hit, 1.0, 0.0).astype(BF)
+        block = halves(kkt[n * tile : (n + 1) * tile, :])
+        taken = taken + dot_n(mark, block[0], NN) + dot_n(mark, block[1], NN)
+    for n in range(y_n):
+        for core in range(2):
+            q = 2 * n + core
+            for part in range(3):
+                picked[core, n, part * width : (part + 1) * width, :] = taken[
+                    part * tile + q * width : part * tile + (q + 1) * width
+                ]
+
     pl.semaphore_wait(barrier, 2 * y_n + z_n + x_n - 3)
 
     def chip_copy(d):
@@ -141,6 +194,8 @@
         chip_copy(d).wait_recv()
         chip_sum[d - 1] = picked[k, lax.rem(y + d, y_n)] + near_in[d]
         y_copy(d).start()
+    inv0 = halves(inverses[0].T)
+    inv1 = halves(inverses[1].T)
     chip_copy(0).wait_recv()
     total = picked[k, y] + near_in[0]
     for d in range(1, y_n):
@@ -324,8 +379,9 @@
             x_copy(strip, i, 1).start()
             wide[x, q, part] = strip[q, part]
 
-    part = jnp.dot(strip[r], moves[...], precision=HI, preferred_element_type=jnp.float32)
-    tile = moves.shape[1] // 3
+    moves = jnp.where((source - first_of(c)) == across, 1.0, 0.0).astype(BF)
+    piece = halves(strip[r])
+    part = dot_n(piece[0], moves, NT) + dot_n(piece[1], moves, NT)
     blocks = ((0, 2), (1, 2), (2, 2), (0, 1), (0, 0), (1, 1))
     stacked = jnp.concatenate(
         [
@@ -365,16 +421,109 @@
         corner_steps(i)
         if i >= lag:
             side_piece(i - lag)
+    for d in range(y_n):
+        twin_copy(corner, d, 1, ch_send, ch_recv).wait_recv()
+
+        @pl.when(not_root)
+        def _():
+            twin_copy(strip, d, 1, h_send, h_recv).wait_recv()
+
+    def along_d(lower_t, panel):
+        pivot = table[:, panel : panel + 1]
+        after = table[:, 2 + panel : 3 + panel]
+        before = table[:, 4 + panel : 5 + panel]
+        return (
+            lower_t * pivot
+            + pltpu.roll(lower_t, tile - 1, 0) * after
+            + pltpu.roll(lower_t, 1, 0) * before
+        )
+
+    def rows_of(ref, part):
+        return jnp.concatenate(
+            [ref[q, part * width : (part + 1) * width, :] for q in range(rows_n)], axis=0
+        )
+
+    block_01 = rows_of(corner, 3)
+    low0_1 = dot3(inv0, halves(block_01))
+    scaled0_1 = along_d(low0_1, 0)
+    scaled0_1_rows = halves(scaled0_1.T)
+    to_partner = [halves(rows_of(corner, part)) for part in range(3)]
+
+    def panels(ref, index):
+        hit = (partner_col - first_of(index)) == columns
+        mark = jnp.where(hit, 1.0, 0.0).astype(BF)
+        keep = 1.0 - jnp.sum(jnp.where(hit, 1.0, 0.0), axis=0, keepdims=True)
+        fixed = [
+            rows_of(ref, part) * keep
+            + dot_n(to_partner[part][0], mark, NN)
+            + dot_n(to_partner[part][1], mark, NN)
+            for part in range(3)
+        ]
+        upper = jnp.where(index == 1, block_01, fixed[0])
+        low0 = dot3(inv0, halves(upper)) * jnp.where(index > 0, 1.0, 0.0)
+        below = fixed[1] - dot3(scaled0_1_rows, halves(low0))
+        low1 = dot3(inv1, halves(below)) * jnp.where(index > 1, 1.0, 0.0)
+        return low0, low1, fixed[2], mark, keep
+
+    low0_c, low1_c, moved_c, mark_c, keep_c = panels(strip, c)
+    scaled0 = along_d(low0_c, 0)
+    scaled1 = along_d(low1_c, 1)
+    scaled0_rows = halves(scaled0.T)
+    scaled1_rows = halves(scaled1.T)
+    moved_rows = halves(moved_c.T)
+    hit_c = (partner_row - first_of(c)) == depths
+    mark_rows = jnp.where(hit_c, 1.0, 0.0).astype(BF)
+
+    def slot_rows(slot):
+        index = r + rows_n * slot
+        low0, low1, moved, mark, keep = panels(wide.at[slot], index)
+        place = pl.ds(pl.multiple_of(slot * tile, tile), tile)
+
+        @pl.when(c > 1)
+        def _():
+            hit = (partner_row - first_of(index)) == depths
+            keep_rows = 1.0 - jnp.sum(jnp.where(hit, 1.0, 0.0), axis=1, keepdims=True)
+            moved_h = halves(moved * keep)
+            change = dot_n(moved_rows[0], mark, NN) + dot_n(moved_rows[1], mark, NN)
+            change = change + dot_n(mark_rows, moved_h[0], NN) + dot_n(mark_rows, moved_h[1], NN)
+            change = change - dot3(scaled0_rows, halves(low0))
+            change = change - dot3(scaled1_rows, halves(low1))
+            value = kkt[place, :] * keep_rows * keep_c + change.T
+            out[place, :] = jnp.where(
+                index == 0, scaled0, jnp.where(index == 1, scaled1, value)
+            )
+
+        @pl.when(c == 0)
+        def _():
+            out[place, :] = jnp.where(index == 0, rows_of(special, 0), low0.T)
+
+        @pl.when(c == 1)
+        def _():
+            first = rows_of(special, 1) - dot3(scaled0_1_rows, halves(low0_1)).T
+            value = jnp.where(index == 1, first, low1.T)
+            out[place, :] = jnp.where(index == 0, scaled0_1, value)
+
     for i in range(pieces - lag, pieces):
         side_piece(i)
 
+    for home in range(2):
+        for n in range(rows_n):
+            if n != home:
+
+                @pl.when((x == 0) & (z == home) & (r == home))
+                def _():
+                    remote(
+                        special.at[n], special.at[n], sp_send, sp_recv.at[n], (n, x, z)
+                    ).wait_recv()
+
+    for step in (0, 1, 3):
+        slot_rows(lax.rem(x + step, x_n))
+    for i in range(pieces):
+        f_copy(i).wait()
+    slot_rows(lax.rem(x + 2, x_n))
+
     for d in range(y_n):
-        @pl.when(not_root)
-        def _():
-            twin_copy(strip, d, 1, h_send, h_recv).wait_recv()
-
         twin_copy(strip, d, 0, h_send, h_recv).wait_send()
-        twin_copy(corner, d, 1, ch_send, ch_recv).wait_recv()
         twin_copy(corner, d, 0, ch_send, ch_recv).wait_send()
         chip_copy(d).wait_send()
     for d in range(1, y_n):
@@ -382,7 +531,6 @@
         gather_copy(strip, d, g_send, g_recv).wait_send()
         gather_copy(corner, d, cr_send, cr_recv).wait_send()
     for i in range(pieces):
-        f_copy(i).wait()
         x_copy(wide.at[x], i, 0).wait_send()
         x_copy(wide.at[x], i, 1).wait_send()
 
@@ -410,40 +558,37 @@
                         special.at[n], special.at[n], sp_send, sp_recv.at[n], (home, x, z)
                     ).wait_send()
 
-                @pl.when(here & (r == home))
-                def _():
-                    remote(
-                        special.at[n], special.at[n], sp_send, sp_recv.at[n], (n, x, z)
-                    ).wait_recv()
-
-
-def exchange(picked, moves, tile, rows_n, x_n):
-    z_n = rows_n
+
+def shards(kkt, swaps, inverses, pivots, couplings, pattern):
+    tile = inverses.shape[1]
+    rows_n = lax.axis_size("row")
+    x_n = lax.axis_size("col_0")
+    z_n = lax.axis_size("col_1")
     y_n = rows_n // 2
     width = tile // rows_n
     depth = 6 * width // z_n
-    f32 = jnp.float32
     dma = pltpu.SemaphoreType.DMA
     vmem = pl.BlockSpec(memory_space=pltpu.VMEM)
     return pl.pallas_call(
-        functools.partial(exchange_kernel, (y_n, x_n, z_n, width)),
-        out_shape=(
-            jax.ShapeDtypeStruct((rows_n, 3 * width, tile), f32),
-            jax.ShapeDtypeStruct((x_n, rows_n, 3 * width, tile), f32),
-            jax.ShapeDtypeStruct((rows_n, 4 * width, tile), f32),
-            jax.ShapeDtypeStruct((rows_n, 2 * width, tile), f32),
-        ),
-        in_specs=[vmem] * 2,
-        out_specs=(vmem,) * 4,
+        functools.partial(step_kernel, (y_n, x_n, z_n, width)),
+        out_shape=jax.ShapeDtypeStruct(kkt.shape, F32),
+        in_specs=[vmem] * 6,
+        out_specs=vmem,
         scratch_shapes=[
-            pltpu.VMEM((y_n, 3 * width, tile), f32),
-            pltpu.VMEM((y_n - 1, 3 * width, tile), f32),
-            pltpu.VMEM((y_n - 1, 3 * width, tile), f32),
-            pltpu.VMEM((z_n, depth, tile), f32),
-            pltpu.VMEM((depth, tile), f32),
-            pltpu.VMEM((z_n - 1, depth, tile), f32),
-            pltpu.VMEM((x_n - 1, depth, tile), f32),
-            pltpu.VMEM((z_n, depth, tile), f32),
+            pltpu.VMEM((128, tile), F32),
+            pltpu.VMEM((2, y_n, 3 * width, tile), F32),
+            pltpu.VMEM((rows_n, 3 * width, tile), F32),
+            pltpu.VMEM((x_n, rows_n, 3 * width, tile), F32),
+            pltpu.VMEM((rows_n, 4 * width, tile), F32),
+            pltpu.VMEM((rows_n, 2 * width, tile), F32),
+            pltpu.VMEM((y_n, 3 * width, tile), F32),
+            pltpu.VMEM((y_n - 1, 3 * width, tile), F32),
+            pltpu.VMEM((y_n - 1, 3 * width, tile), F32),
+            pltpu.VMEM((z_n, depth, tile), F32),
+            pltpu.VMEM((depth, tile), F32),
+            pltpu.VMEM((z_n - 1, depth, tile), F32),
+            pltpu.VMEM((x_n - 1, depth, tile), F32),
+            pltpu.VMEM((z_n, depth, tile), F32),
             dma((y_n,)),
             dma((y_n,)),
             dma((y_n - 1,)),
@@ -472,185 +617,7 @@
             dma((rows_n,)),
         ],
         compiler_params=pltpu.CompilerParams(collective_id=0, has_side_effects=True),
-    )(picked, moves)
-
-
-BF = jnp.bfloat16
-
-
-def halves(a):
-    high = a.astype(BF)
-    return high, (a - high.astype(jnp.float32)).astype(BF)
-
-
-def dot_n(a, b, dims):
-    return lax.dot_general(a, b, (dims, ((), ())), preferred_element_type=jnp.float32)
-
-
-def dot3(a, b, dims):
-    return dot_n(a[0], b[0], dims) + (dot_n(a[0], b[1], dims) + dot_n(a[1], b[0], dims))
-
-
-NN = ((1,), (0,))
-
-
-def update_kernel(
-    kkt,
-    wide,
-    strip,
-    corner,
-    special,
-    inverses,
-    pivots,
-    couplings,
-    pattern,
-    partner_col,
-    partner_row,
-    out,
-    coef,
-):
-    x_n, rows_n, deep, tile = wide.shape
-    width = deep // 3
-    r = lax.axis_index("row")
-    c = lax.axis_index("col_0") * lax.axis_size("col_1") + lax.axis_index("col_1")
-    lanes = lax.broadcasted_iota(jnp.int32, (2, tile), 1)
-    links = couplings[...] * pattern[...].astype(jnp.float32)
-    links = jnp.where(lanes == tile - 1, 0.0, links)
-    coef[...] = jnp.zeros_like(coef)
-    coef[0:2, :] = pivots[...]
-    coef[2:4, :] = links
-    coef[4:6, :] = jnp.where(lanes == 0, 0.0, pltpu.roll(links, 1, 1))
-    table = coef[...].T
-
-    def along_d(lower_t, panel):
-        pivot = table[:, panel : panel + 1]
-        after = table[:, 2 + panel : 3 + panel]
-        before = table[:, 4 + panel : 5 + panel]
-        return (
-            lower_t * pivot
-            + pltpu.roll(lower_t, tile - 1, 0) * after
-            + pltpu.roll(lower_t, 1, 0) * before
-        )
-
-    def rows_of(ref, part):
-        return jnp.concatenate(
-            [ref[q, part * width : (part + 1) * width, :] for q in range(rows_n)], axis=0
-        )
-
-    tiles = [r + rows_n * slot for slot in range(x_n)] + [c]
-    inv0 = halves(inverses[0].T)
-    inv1 = halves(inverses[1].T)
-    block_01 = rows_of(corner, 3)
-    low0_1 = dot3(inv0, halves(block_01), NN)
-    scaled0_1 = along_d(low0_1, 0)
-    scaled0_1_rows = halves(scaled0_1.T)
-    to_partner = [halves(rows_of(corner, part)) for part in range(3)]
-    columns = lax.broadcasted_iota(jnp.int32, (tile, tile), 1)
-    depths = lax.broadcasted_iota(jnp.int32, (tile, tile), 0)
-
-    def panels(n):
-        ref = strip if n == x_n else wide.at[n]
-        index = tiles[n]
-        hit = (partner_col[...] - index * tile) == columns
-        mark = jnp.where(hit, 1.0, 0.0).astype(BF)
-        keep = 1.0 - jnp.sum(jnp.where(hit, 1.0, 0.0), axis=0, keepdims=True)
-        fixed = [
-            rows_of(ref, part) * keep
-            + dot_n(to_partner[part][0], mark, NN)
-            + dot_n(to_partner[part][1], mark, NN)
-            for part in range(3)
-        ]
-        upper = jnp.where(index == 1, block_01, fixed[0])
-        low0 = dot3(inv0, halves(upper), NN) * jnp.where(index > 0, 1.0, 0.0)
-        below = fixed[1] - dot3(scaled0_1_rows, halves(low0), NN)
-        low1 = dot3(inv1, halves(below), NN) * jnp.where(index > 1, 1.0, 0.0)
-        return low0, low1, fixed[2], mark, keep
-
-    low0_c, low1_c, moved_c, mark_c, keep_c = panels(x_n)
-    scaled0 = along_d(low0_c, 0)
-    scaled1 = along_d(low1_c, 1)
-    scaled0_rows = halves(scaled0.T)
-    scaled1_rows = halves(scaled1.T)
-    moved_rows = halves(moved_c.T)
-    hit_c = (partner_row[...] - c * tile) == depths
-    mark_rows = jnp.where(hit_c, 1.0, 0.0).astype(BF)
-
-    for n in range(x_n):
-        low0, low1, moved, mark, keep = panels(n)
-        place = slice(n * tile, (n + 1) * tile)
-
-        @pl.when(c > 1)
-        def _():
-            hit = (partner_row[...] - tiles[n] * tile) == depths
-            keep_rows = 1.0 - jnp.sum(jnp.where(hit, 1.0, 0.0), axis=1, keepdims=True)
-            across = halves(moved * keep)
-            change = dot_n(moved_rows[0], mark, NN) + dot_n(moved_rows[1], mark, NN)
-            change = change + dot_n(mark_rows, across[0], NN) + dot_n(mark_rows, across[1], NN)
-            change = change - dot3(scaled0_rows, halves(low0), NN)
-            change = change - dot3(scaled1_rows, halves(low1), NN)
-            value = kkt[place, :] * keep_rows * keep_c + change.T
-            if n == 0:
-                value = jnp.where(r == 0, scaled0, jnp.where(r == 1, scaled1, value))
-            out[place, :] = value
-
-        @pl.when(c == 0)
-        def _():
-            value = low0.T
-            if n == 0:
-                value = jnp.where(r == 0, rows_of(special, 0), value)
-            out[place, :] = value
-
-        @pl.when(c == 1)
-        def _():
-            value = low1.T
-            if n == 0:
-                first = rows_of(special, 1) - dot3(scaled0_1_rows, halves(low0_1), NN).T
-                value = jnp.where(r == 0, scaled0_1, jnp.where(r == 1, first, value))
-            out[place, :] = value
-
-
-def update(kkt, wide, strip, corner, special, inverses, pivots, couplings, pattern, partner):
-    tile = kkt.shape[1]
-    vmem = pl.BlockSpec(memory_space=pltpu.VMEM)
-    return pl.pallas_call(
-        update_kernel,
-        out_shape=jax.ShapeDtypeStruct(kkt.shape, jnp.float32),
-        in_specs=[vmem] * 11,
-        out_specs=vmem,
-        scratch_shapes=[pltpu.VMEM((128, tile), jnp.float32)],
-    )(
-        kkt,
-        wide,
-        strip,
-        corner,
-        special,
-        inverses,
-        pivots,
-        couplings,
-        pattern,
-        partner[:, None],
-        partner[None, :],
-    )
-
-
-def shards(kkt, swaps, inverses, pivots, couplings, pattern):
-    tile = inverses.shape[1]
-    row_groups = lax.axis_size("row")
-    x_size = lax.axis_size("col_0")
-    z_size = lax.axis_size("col_1")
-    row_index = lax.axis_index("row")
-    col_index = lax.axis_index(COL)
-    rows, source, sliced, partner = plan(swaps, tile, row_groups)
-    flat = sliced.reshape(-1)
-    owned = flat // tile % row_groups == row_index
-    taken = jnp.take(kkt, flat // tile // row_groups * tile + flat % tile, axis=0)
-    picked = jnp.where(owned[:, None], taken, 0.0).reshape(2, row_groups // 2, -1, tile)
-    moves = hits(source, col_index * tile, tile).T
-    strip, wide, corner, special = exchange(picked, moves, tile, row_groups, x_size)
-
-    return update(
-        kkt, wide, strip, corner, special, inverses, pivots, couplings, pattern, partner
-    )
+    )(kkt, swaps.reshape(4, -1), inverses, pivots, couplings, pattern)
 
 
 def solution(mesh):

time: 99.9 us -> 82.8 us (0.83); the launches traced: 97.9 us -> 82.6 us
  Pallas kernels: 88.3 us -> 80.3 us
  other arithmetic: 3.69 us -> 0 us
  local copies, waits for them, and re-layouts: 5.84 us -> 2.26 us
    pallas_call x2 -> x1, Pallas kernels: 88.3 us -> 80.3 us  [shards(): pl.pallas_call(functools.partial(step_kernel, (y_n, x_n, z_n, width)), ou...]
    gather x1 -> x0, local copies, waits for them, and re-layouts: 3.33 us -> none  [shards(): jnp.take(kkt, flat // tile // row_groups * tile + flat % tile, axis=0)]
    unnamed x2 -> x1, local copies, waits for them, and re-layouts: 0.01 us -> 2.26 us
    select_n x5 -> x0, other arithmetic: 1.23 us -> none  [the longest x1 1.15 us: shards(): jnp.where(owned[:, None], taken, 0.0).reshape(2, row_groups // 2, -1, tile)]
    convert_element_type x1 -> x0, other arithmetic: 1.03 us -> none  [hits(): (rows[:, None] == first + jnp.arange(tile, dtype=jnp.int32)[None, :]).ast...]
where the time goes in v5:
time: 82.8 us; the launch traced here: 82.6 us
  Pallas kernels  80.3 us (97%)
  local copies, waits for them, and re-layouts  2.26 us (3%)
    pallas_call x1, Pallas kernels, shards(): pl.pallas_call(functools.partial(step_kernel, (y_n, x_n, z_n, width)), ou...  80.3 us
    unnamed x1, local copies, waits for them, and re-layouts  2.26 us

profile of v5, /device:TPU:18, one launch (start us, length us, event | category | flops | bytes accessed | tf_op | source)
XLA Modules:
  0.0 82.6 jit_solution(12118403627520799340)
XLA Ops:
  0.0 80.3 %shard_map.64 = f32[1024,256]{1,0:T(8,128)} custom-call(f32[1024,256]{1,0:T(8,128)} %kkt.1, s32[4,128]{1,0:T(4,128)} %bitcast.1, f32[2,256,256]{2,1,0:T(8,128)} %inverses.1, f32[2,256]{1,0:T(2,128)} %pivots.1, f32[2,256]{1,0:T(2,128)} %couplings.1, s32[2,256]{1,0:T(2,128)} %pattern.1), custom_call_target="tpu_custom_call" | custom-call | tf_op jit(solution)/shard_map/pallas_call | solution.py:572
  80.4 2.3 %copy.8 = f32[1024,256]{1,0:T(8,128)} copy(f32[1024,256]{1,0:T(8,128)} %shard_map.64) | data formatting | bytes 2097152

commit v6 on v5

--- a/solution.py
+++ b/solution.py
@@ -182,9 +182,16 @@
         n = lax.rem(y + d, y_n)
         return remote(picked.at[1 - k, n], near_in.at[d], p_send.at[d], p_recv.at[d], twin)
 
-    def y_copy(d):
+    cut = 3 * width // 2
+
+    def y_copy(d, half):
+        part = pl.ds(half * cut, cut)
         return remote(
-            chip_sum.at[d - 1], far_in.at[d - 1], r_send.at[d - 1], r_recv.at[d - 1], y_peer(d)
+            chip_sum.at[d - 1, part],
+            far_in.at[d - 1, part],
+            r_send.at[half, d - 1],
+            r_recv.at[half, d - 1],
+            y_peer(d),
         )
 
     order = [2, 1, 3, 0] if y_n == 4 else list(range(1, y_n)) + [0]
@@ -193,15 +200,12 @@
     for d in order[:-1]:
         chip_copy(d).wait_recv()
         chip_sum[d - 1] = picked[k, lax.rem(y + d, y_n)] + near_in[d]
-        y_copy(d).start()
+        y_copy(d, 0).start()
+    for d in order[:-1]:
+        y_copy(d, 1).start()
     inv0 = halves(inverses[0].T)
     inv1 = halves(inverses[1].T)
     chip_copy(0).wait_recv()
-    total = picked[k, y] + near_in[0]
-    for d in range(1, y_n):
-        y_copy(d).wait_recv()
-        total = total + far_in[d - 1]
-    strip[r] = total
 
     def gather_copy(ref, d, send, recv):
         return remote(ref.at[r], ref.at[r], send.at[d - 1], recv.at[d - 1], y_peer(d))
@@ -213,10 +217,6 @@
     def twin_copy(ref, d, flip, send, recv):
         q = owner(d, flip)
         return remote(ref.at[q], ref.at[q], send.at[d], recv.at[d], twin)
-
-    for d in range(1, y_n):
-        gather_copy(strip, d, g_send, g_recv).start()
-    twin_copy(strip, 0, 0, h_send, h_recv).start()
 
     offset = lax.rem(z - r + z_n, z_n)
     half = z_n // 2
@@ -229,16 +229,20 @@
     is_near = reach <= 1
     is_mid = reach == 2
     is_far = reach > 2
-    cut = 3 * width // 2
     if y_n == 4:
         turn = [(0, 0), (0, 1), (1, 0), (3, 0), (1, 1), (3, 1), (2, 0), (2, 1)]
     else:
         turn = [(d, flip) for d in range(y_n) for flip in range(2)]
-    pieces = 2 * rows_n
+    spans = []
+    for e in range(rows_n):
+        count_e = 4 if e in (0, rows_n - 1) else 2
+        depth_e = 3 * width // count_e
+        spans += [(e, n * depth_e, depth_e) for n in range(count_e)]
+    pieces = len(spans)
 
     def spot(i):
-        q = owner(*turn[i // 2])
-        return q, pl.ds((i % 2) * cut, cut)
+        e, start, size = spans[i]
+        return owner(*turn[e]), pl.ds(start, size)
 
     def z_copy(src, i, slot, step):
         q, part = spot(i)
@@ -264,11 +268,11 @@
 
     def own_piece(i):
         q, part = spot(i)
-        d, flip = turn[i // 2]
+        d, flip = turn[spans[i][0]]
 
         @pl.when(is_root)
         def _():
-            if i % 2 == 0 and flip == 1:
+            if spans[i][1] == 0 and flip == 1:
                 twin_copy(strip, d, 1, h_send, h_recv).wait_recv()
             z_copy(strip, i, 0, 1).start()
             z_copy(strip, i, 1, z_n - 1).start()
@@ -356,8 +360,9 @@
             twin_copy(corner, d, 0, ch_send, ch_recv).start()
 
     steps = [corner_z, corner_x, corner_back, corner_twin]
-    spots = {True: [[3, 5, 11, 14], [1, 3, 9, 13], [-1, -1, 6, 11]], False: [[2, 3, 5, 6]] * 3}
-    spots = spots[pieces == 16]
+    spots = [[5, 7, 13, 15], [3, 5, 11, 15], [-1, -1, 8, 13]]
+    if y_n != 4:
+        spots = [[2, 3, 5, 6]] * 3
 
     def corner_steps(i):
         for kind, at in zip((is_near, is_mid, is_far), spots):
@@ -369,15 +374,27 @@
                         if place == i:
                             step()
 
-    @pl.when(is_root)
-    def _():
-        for i in range(2):
-            q, part = spot(i)
-            z_copy(strip, i, 0, 1).start()
-            z_copy(strip, i, 1, z_n - 1).start()
-            x_copy(strip, i, 0).start()
-            x_copy(strip, i, 1).start()
-            wide[x, q, part] = strip[q, part]
+    for half in range(2):
+        rows_h = slice(half * cut, (half + 1) * cut)
+        total = picked[k, y, rows_h, :] + near_in[0, rows_h, :]
+        for d in range(1, y_n):
+            y_copy(d, half).wait_recv()
+            total = total + far_in[d - 1, rows_h, :]
+        strip[r, rows_h, :] = total
+
+        @pl.when(is_root)
+        def _():
+            for i in (2 * half, 2 * half + 1):
+                q, part = spot(i)
+                z_copy(strip, i, 0, 1).start()
+                z_copy(strip, i, 1, z_n - 1).start()
+                x_copy(strip, i, 0).start()
+                x_copy(strip, i, 1).start()
+                wide[x, q, part] = strip[q, part]
+
+    for d in range(1, y_n):
+        gather_copy(strip, d, g_send, g_recv).start()
+    twin_copy(strip, 0, 0, h_send, h_recv).start()
 
     moves = jnp.where((source - first_of(c)) == across, 1.0, 0.0).astype(BF)
     piece = halves(strip[r])
@@ -401,9 +418,9 @@
         twin_copy(strip, d, 0, h_send, h_recv).start()
 
     corner_steps(-1)
-    lag = 2
+    lag = 5
     for i in range(pieces):
-        if i > 1:
+        if i > 3:
             own_piece(i)
         else:
 
@@ -503,9 +520,6 @@
             value = jnp.where(index == 1, first, low1.T)
             out[place, :] = jnp.where(index == 0, scaled0_1, value)
 
-    for i in range(pieces - lag, pieces):
-        side_piece(i)
-
     for home in range(2):
         for n in range(rows_n):
             if n != home:
@@ -516,7 +530,13 @@
                         special.at[n], special.at[n], sp_send, sp_recv.at[n], (n, x, z)
                     ).wait_recv()
 
-    for step in (0, 1, 3):
+    side_piece(pieces - 5)
+    side_piece(pieces - 4)
+    slot_rows(x)
+    for i in range(pieces - 3, pieces):
+        side_piece(i)
+
+    for step in (1, 3):
         slot_rows(lax.rem(x + step, x_n))
     for i in range(pieces):
         f_copy(i).wait()
@@ -527,7 +547,8 @@
         twin_copy(corner, d, 0, ch_send, ch_recv).wait_send()
         chip_copy(d).wait_send()
     for d in range(1, y_n):
-        y_copy(d).wait_send()
+        y_copy(d, 0).wait_send()
+        y_copy(d, 1).wait_send()
         gather_copy(strip, d, g_send, g_recv).wait_send()
         gather_copy(corner, d, cr_send, cr_recv).wait_send()
     for i in range(pieces):
@@ -591,18 +612,18 @@
             pltpu.VMEM((z_n, depth, tile), F32),
             dma((y_n,)),
             dma((y_n,)),
-            dma((y_n - 1,)),
-            dma((y_n - 1,)),
+            dma((2, y_n - 1)),
+            dma((2, y_n - 1)),
             dma((y_n - 1,)),
             dma((y_n - 1,)),
             dma((y_n,)),
             dma((y_n,)),
-            dma((2, 2 * rows_n)),
-            dma((2 * rows_n,)),
-            dma((2, 2 * rows_n)),
-            dma((2, 2 * rows_n)),
-            dma((2 * rows_n,)),
-            dma((2 * rows_n,)),
+            dma((2, 2 * rows_n + 4)),
+            dma((2 * rows_n + 4,)),
+            dma((2, 2 * rows_n + 4)),
+            dma((2, 2 * rows_n + 4)),
+            dma((2 * rows_n + 4,)),
+            dma((2 * rows_n + 4,)),
             dma((z_n - 1,)),
             dma((z_n - 1,)),
             dma((x_n - 1,)),
@@ -616,7 +637,9 @@
             dma,
             dma((rows_n,)),
         ],
-        compiler_params=pltpu.CompilerParams(collective_id=0, has_side_effects=True),
+        compiler_params=pltpu.CompilerParams(
+            collective_id=0, has_side_effects=True, vmem_limit_bytes=32 << 20
+        ),
     )(kkt, swaps.reshape(4, -1), inverses, pivots, couplings, pattern)
 
 

time: 82.8 us -> 82.6 us (level)
  Pallas kernels: 80.3 us -> 76.3 us
  local copies, waits for them, and re-layouts: 2.26 us -> 5.96 us
    pallas_call x1, Pallas kernels: 80.3 us -> 76.3 us  [shards(): pl.pallas_call(functools.partial(step_kernel, (y_n, x_n, z_n, width)), ou...]
    unnamed x1 -> x13, local copies, waits for them, and re-layouts: 2.26 us -> 5.96 us
where the time goes in v6:
time: 82.6 us; the launch traced here: 82.3 us
  Pallas kernels  76.3 us (92%)
  local copies, waits for them, and re-layouts  5.96 us (7%)
    pallas_call x1, Pallas kernels, shards(): pl.pallas_call(functools.partial(step_kernel, (y_n, x_n, z_n, width)), ou...  76.3 us
    unnamed x13, local copies, waits for them, and re-layouts  5.96 us

profile of v6, /device:TPU:18, one launch (start us, length us, event | category | flops | bytes accessed | tf_op | source)
XLA Modules:
  0.0 82.3 jit_solution(3388059743385833853)
XLA Ops:
  0.0 0.0 copy-start
  0.0 1.2 %copy-done = f32[1024,256]{1,0:T(8,128)S(1)} copy-done((f32[1024,256]{1,0:T(8,128)S(1)}, f32[1024,256]{1,0:T(8,128)}, u32[]{:S(2)}) %copy-start) | copy-done | bytes 1048600
  1.2 0.0 copy-start.1
  1.2 1.0 %copy-done.1 = f32[2,256,256]{2,1,0:T(8,128)S(1)} copy-done((f32[2,256,256]{2,1,0:T(8,128)S(1)}, f32[2,256,256]{2,1,0:T(8,128)}, u32[]{:S(2)}) %copy-start.1) | copy-done | bytes 524312
  2.3 0.0 copy-start.2
  2.3 0.7 copy-done.2
  3.0 0.0 copy-start.3
  3.0 0.7 copy-done.3
  3.6 0.0 copy-start.4
  3.6 0.7 copy-done.4
  4.3 0.0 copy-start.5
  4.3 0.7 copy-done.5
  5.0 76.3 %shard_map.64 = f32[1024,256]{1,0:T(8,128)S(1)} custom-call(f32[1024,256]{1,0:T(8,128)S(1)} %copy-done, s32[4,128]{1,0:T(4,128)S(1)} %bitcast.1, f32[2,256,256]{2,1,0:T(8,128)S(1)} %copy-done.1, f32[2,256]{1,0:T(2,128)S(1)} %copy-done.3, f32[2,256]{1,0:T(2,128)S(1)} %copy-done.4, s32[2,256]{1,0:T(2,128)S(1)} %copy-done.5), custom_call_target="tpu_custom_call" | custom-call | tf_op jit(solution)/shard_map/pallas_call | solution.py:593
  81.3 1.0 %copy.8 = f32[1024,256]{1,0:T(8,128)} copy(f32[1024,256]{1,0:T(8,128)S(1)} %shard_map.64) | data formatting | bytes 2097152
Async XLA Ops:
  0.0 1.2 %copy-start = (f32[1024,256]{1,0:T(8,128)S(1)}, f32[1024,256]{1,0:T(8,128)}, u32[]{:S(2)}) copy-start(f32[1024,256]{1,0:T(8,128)} %kkt.1) | copy-start | bytes 3145732
  1.2 1.0 %copy-start.1 = (f32[2,256,256]{2,1,0:T(8,128)S(1)}, f32[2,256,256]{2,1,0:T(8,128)}, u32[]{:S(2)}) copy-start(f32[2,256,256]{2,1,0:T(8,128)} %inverses.1) | copy-start | bytes 1572868
  2.3 0.7 copy-start.2
  3.0 0.7 copy-start.3
  3.6 0.7 copy-start.4
  4.3 0.7 copy-start.5

commit v7 on v6

--- a/solution.py
+++ b/solution.py
@@ -48,13 +48,20 @@
 
 def step_kernel(
     sizes,
+    kkt_hbm,
+    swaps_hbm,
+    inverses_hbm,
+    pivots_hbm,
+    couplings_hbm,
+    pattern_hbm,
+    out,
     kkt,
     swaps,
     inverses,
     pivots,
     couplings,
     pattern,
-    out,
+    in_sem,
     coef,
     picked,
     strip,
@@ -118,6 +125,21 @@
         core = k if flip == 0 else 1 - k
         return 2 * lax.rem(y - d + y_n, y_n) + core
 
+    loads = [
+        pltpu.make_async_copy(src, dst, in_sem.at[n])
+        for n, (src, dst) in enumerate(
+            (
+                (swaps_hbm, swaps),
+                (pivots_hbm, pivots),
+                (couplings_hbm, couplings),
+                (pattern_hbm, pattern),
+                (kkt_hbm, kkt),
+                (inverses_hbm, inverses),
+            )
+        )
+    ]
+    for load in loads:
+        load.start()
     barrier = pltpu.get_barrier_semaphore()
     pl.semaphore_signal(barrier, inc=1, device_id=twin, device_id_type=MESH)
     for d in range(1, y_n):
@@ -132,6 +154,8 @@
 
     c = x * z_n + z
     tile = inverses.shape[1]
+    for load in loads[:4]:
+        load.wait()
     count = tile // 2
     lanes = lax.broadcasted_iota(jnp.int32, (2, tile), 1)
     links = couplings[...] * pattern[...].astype(F32)
@@ -162,6 +186,7 @@
     def first_of(index):
         return (index * tile).astype(F32)
 
+    loads[4].wait()
     taken = jnp.zeros((3 * tile, tile), F32)
     for n in range(x_n):
         hit = (source - first_of(r + rows_n * n)) == across
@@ -203,6 +228,7 @@
         y_copy(d, 0).start()
     for d in order[:-1]:
         y_copy(d, 1).start()
+    loads[5].wait()
     inv0 = halves(inverses[0].T)
     inv1 = halves(inverses[1].T)
     chip_copy(0).wait_recv()
@@ -593,9 +619,16 @@
     return pl.pallas_call(
         functools.partial(step_kernel, (y_n, x_n, z_n, width)),
         out_shape=jax.ShapeDtypeStruct(kkt.shape, F32),
-        in_specs=[vmem] * 6,
+        in_specs=[pl.BlockSpec(memory_space=pltpu.HBM)] * 6,
         out_specs=vmem,
         scratch_shapes=[
+            pltpu.VMEM(kkt.shape, F32),
+            pltpu.VMEM((4, tile // 2), jnp.int32),
+            pltpu.VMEM(inverses.shape, F32),
+            pltpu.VMEM(pivots.shape, F32),
+            pltpu.VMEM(couplings.shape, F32),
+            pltpu.VMEM(pattern.shape, jnp.int32),
+            dma((6,)),
             pltpu.VMEM((128, tile), F32),
             pltpu.VMEM((2, y_n, 3 * width, tile), F32),
             pltpu.VMEM((rows_n, 3 * width, tile), F32),
@@ -637,9 +670,7 @@
             dma,
             dma((rows_n,)),
         ],
-        compiler_params=pltpu.CompilerParams(
-            collective_id=0, has_side_effects=True, vmem_limit_bytes=32 << 20
-        ),
+        compiler_params=pltpu.CompilerParams(collective_id=0, has_side_effects=True),
     )(kkt, swaps.reshape(4, -1), inverses, pivots, couplings, pattern)
 
 

time: 82.6 us -> 79.6 us (0.964)
  local copies, waits for them, and re-layouts: 5.96 us -> 2.26 us
    unnamed x13 -> x1, local copies, waits for them, and re-layouts: 5.96 us -> 2.26 us
where the time goes in v7:
time: 79.6 us; the launch traced here: 79.4 us
  Pallas kernels  77.1 us (97%)
  local copies, waits for them, and re-layouts  2.26 us (3%)
    pallas_call x1, Pallas kernels, shards(): pl.pallas_call(functools.partial(step_kernel, (y_n, x_n, z_n, width)), ou...  77.1 us
    unnamed x1, local copies, waits for them, and re-layouts  2.26 us

profile of v7, /device:TPU:18, one launch (start us, length us, event | category | flops | bytes accessed | tf_op | source)
XLA Modules:
  0.0 79.4 jit_solution(22019664248205337)
XLA Ops:
  0.0 77.1 %shard_map.64 = f32[1024,256]{1,0:T(8,128)} custom-call(f32[1024,256]{1,0:T(8,128)} %kkt_hbm.1, s32[4,128]{1,0:T(4,128)} %bitcast.1, f32[2,256,256]{2,1,0:T(8,128)} %inverses_hbm.1, f32[2,256]{1,0:T(2,128)} %pivots_hbm.1, f32[2,256]{1,0:T(2,128)} %couplings_hbm.1, s32[2,256]{1,0:T(2,128)} %pattern_hbm.1), custom_call_target="tpu_custom_call" | custom-call | tf_op jit(solution)/shard_map/pallas_call | solution.py:619
  77.1 2.3 %copy.8 = f32[1024,256]{1,0:T(8,128)} copy(f32[1024,256]{1,0:T(8,128)} %shard_map.64) | data formatting | bytes 2097152

commit v8 on v7

--- a/solution.py
+++ b/solution.py
@@ -386,7 +386,7 @@
             twin_copy(corner, d, 0, ch_send, ch_recv).start()
 
     steps = [corner_z, corner_x, corner_back, corner_twin]
-    spots = [[5, 7, 13, 15], [3, 5, 11, 15], [-1, -1, 8, 13]]
+    spots = [[5, 7, 13, 15], [3, 5, 11, 15], [3, 5, 9, 13]]
     if y_n != 4:
         spots = [[2, 3, 5, 6]] * 3
 
@@ -439,27 +439,34 @@
     for d in range(1, z_n):
         share_copy(d).start()
 
+    def pass_on(i):
+        z_copy(wide.at[x], i, 0, ahead).wait_recv()
+
+        @pl.when(passes)
+        def _():
+            z_copy(wide.at[x], i, 0, ahead).start()
+
+        x_copy(wide.at[x], i, 0).start()
+        x_copy(wide.at[x], i, 1).start()
+
+    @pl.when(not_root & (reach <= 2))
+    def _():
+        for i in range(4):
+            pass_on(i)
+
     for d in (1, 3, 2) if y_n == 4 else range(1, y_n):
         gathered(strip, d, g_send, g_recv).wait_recv()
         twin_copy(strip, d, 0, h_send, h_recv).start()
 
-    corner_steps(-1)
     lag = 5
     for i in range(pieces):
         if i > 3:
             own_piece(i)
         else:
 
-            @pl.when(not_root)
+            @pl.when(reach > 2)
             def _():
-                z_copy(wide.at[x], i, 0, ahead).wait_recv()
-
-                @pl.when(passes)
-                def _():
-                    z_copy(wide.at[x], i, 0, ahead).start()
-
-                x_copy(wide.at[x], i, 0).start()
-                x_copy(wide.at[x], i, 1).start()
+                pass_on(i)
 
         corner_steps(i)
         if i >= lag:
@@ -532,19 +539,18 @@
             change = change - dot3(scaled0_rows, halves(low0))
             change = change - dot3(scaled1_rows, halves(low1))
             value = kkt[place, :] * keep_rows * keep_c + change.T
-            out[place, :] = jnp.where(
-                index == 0, scaled0, jnp.where(index == 1, scaled1, value)
-            )
+            value = jnp.where(index == 0, scaled0, jnp.where(index == 1, scaled1, value))
+            out[place, :] = value - kkt[place, :]
 
         @pl.when(c == 0)
         def _():
-            out[place, :] = jnp.where(index == 0, rows_of(special, 0), low0.T)
+            out[place, :] = jnp.where(index == 0, rows_of(special, 0), low0.T) - kkt[place, :]
 
         @pl.when(c == 1)
         def _():
             first = rows_of(special, 1) - dot3(scaled0_1_rows, halves(low0_1)).T
             value = jnp.where(index == 1, first, low1.T)
-            out[place, :] = jnp.where(index == 0, scaled0_1, value)
+            out[place, :] = jnp.where(index == 0, scaled0_1, value) - kkt[place, :]
 
     for home in range(2):
         for n in range(rows_n):
@@ -616,7 +622,7 @@
     depth = 6 * width // z_n
     dma = pltpu.SemaphoreType.DMA
     vmem = pl.BlockSpec(memory_space=pltpu.VMEM)
-    return pl.pallas_call(
+    change = pl.pallas_call(
         functools.partial(step_kernel, (y_n, x_n, z_n, width)),
         out_shape=jax.ShapeDtypeStruct(kkt.shape, F32),
         in_specs=[pl.BlockSpec(memory_space=pltpu.HBM)] * 6,
@@ -672,6 +678,7 @@
         ],
         compiler_params=pltpu.CompilerParams(collective_id=0, has_side_effects=True),
     )(kkt, swaps.reshape(4, -1), inverses, pivots, couplings, pattern)
+    return kkt + change
 
 
 def solution(mesh):

time: 79.6 us -> 79.4 us (level)
  other arithmetic: 0 us -> 2.33 us
  local copies, waits for them, and re-layouts: 2.26 us -> 0.01 us
    add x0 -> x1, other arithmetic: none -> 2.33 us  [shards(): return kkt + change]
    unnamed x1 -> x2, local copies, waits for them, and re-layouts: 2.26 us -> 0.01 us
where the time goes in v8:
time: 79.4 us; the launch traced here: 79.2 us
  Pallas kernels  76.8 us (97%)
  other arithmetic  2.33 us (3%)
    pallas_call x1, Pallas kernels, shards(): pl.pallas_call(functools.partial(step_kernel, (y_n, x_n, z_n, width)), ou...  76.8 us
    add x1, other arithmetic, shards(): return kkt + change  2.33 us

profile of v8, /device:TPU:18, one launch (start us, length us, event | category | flops | bytes accessed | tf_op | source)
XLA Modules:
  0.0 79.2 jit_solution(3887389455888824379)
XLA Ops:
  0.0 0.0 copy-start
  0.0 76.8 %shard_map.64 = f32[1024,256]{1,0:T(8,128)} custom-call(f32[1024,256]{1,0:T(8,128)} %kkt_hbm.1, s32[4,128]{1,0:T(4,128)} %bitcast.1, f32[2,256,256]{2,1,0:T(8,128)} %inverses_hbm.1, f32[2,256]{1,0:T(2,128)} %pivots_hbm.1, f32[2,256]{1,0:T(2,128)} %couplings_hbm.1, s32[2,256]{1,0:T(2,128)} %pattern_hbm.1), custom_call_target="tpu_custom_call" | custom-call | tf_op jit(solution)/shard_map/pallas_call | solution.py:625
  76.8 0.0 copy-done
  76.8 2.3 %add.3 = f32[1024,256]{1,0:T(8,128)} add(f32[1024,256]{1,0:T(8,128)S(1)} %copy-done, f32[1024,256]{1,0:T(8,128)} %shard_map.64) | non-fusion elementwise | flops 262144 | bytes 3145728 | tf_op jit(solution)/shard_map/add | solution.py:681
Async XLA Ops:
  0.0 76.8 %copy-start = (f32[1024,256]{1,0:T(8,128)S(1)}, f32[1024,256]{1,0:T(8,128)}, u32[]{:S(2)}) copy-start(f32[1024,256]{1,0:T(8,128)} %kkt_hbm.1) | copy-start | bytes 3145732
